TPU v7x, 256 devices: a whole 4x4x8 slice. The times are simulated.
256 devices in a mesh: gx: 8 (over z_lo, y), gy: 4 (over x), gz: 8 (over z_hi, core).
Axes of the slice: x: 4, y: 4, z: 8 (z_hi: 4, z_lo: 2; z = z_hi * 2 + z_lo), core: 2. Of those that a mesh axis runs over, the one named last changes fastest.
Arguments:
- coordinates: float32 [8, 4, 8, 3, 16, 128], P('gx', 'gy', 'gz'), may hold values from -8 to 168
- neighbours: int32 [8, 4, 8, 16, 128], P('gx', 'gy', 'gz'), may hold values from 0 to 991, as said below
- pair_index: int32 [8, 4, 8, 4, 15360], P('gx', 'gy', 'gz'), may hold values from 0 to 127, as said below
- pair_live: int32 [8, 4, 8, 15360], P('gx', 'gy', 'gz'), may hold values 0 or 1
- basis: bfloat16 [8, 4, 8, 128, 1536], P('gx', 'gy', 'gz'), may hold values from -50 to 50
Outputs:
- next_basis: float32 [8, 4, 8, 128, 1536], P('gx', 'gy', 'gz')
- ritz_matrix: float32 [256, 256], replicated
Inputs may be any that keep to these rules, and one draw needn't show every extreme that they name: neighbours[x, y, z, 0, f] = 864 + f. Any other entry c < 864 names frame c % 32 of the domain offset by (c // 32 // 9 - 1, c // 32 // 3 % 3 - 1, c // 32 % 3 - 1), which lies in the grid and is not the domain itself; an entry c >= 864 names the domain's own frame c - 864, never the row's frame f. `pair_index`: row 0 holds a frame f < 128, row 1 a slot 1 to 15, rows 2 and 3 atoms below 16.
All inputs are finite; a program needn't handle non-finite values. No bound on the sum of `pair_live` on one device may be relied on, other than what follows from the above.
Results may differ from a plain program's by a relative error of at most 0.0003.
Values may be sent and summed in bfloat16 or wider, within the bound.
A program may use at most 128 MiB of HBM per device.

v0:
```python
import jax
import jax.numpy as jnp
from jax import lax
from jax.sharding import Mesh
from jax.sharding import PartitionSpec as P

GX = ("gx_0", "gx_1")
GZ = ("gz_0", "gz_1")


stiffness = 0.01


def padded(cells, sides, width, closed):
    for axis, dim in sides:
        count = lax.axis_size(axis)
        ends = count if closed else count - 1
        head = lax.slice_in_dim(cells, 0, width, axis=dim)
        tail = lax.slice_in_dim(cells, cells.shape[dim] - width, cells.shape[dim], axis=dim)
        cells = jnp.concatenate(
            [
                lax.ppermute(tail, axis, [(i, (i + 1) % count) for i in range(ends)]),
                cells,
                lax.ppermute(head, axis, [((i + 1) % count, i) for i in range(ends)]),
            ],
            axis=dim,
        )
    return cells


def rows_for(lines, size):
    spare = -len(lines) % size
    return jnp.pad(lines, [(0, spare)] + [(0, 0)] * (lines.ndim - 1))


def sum_in_two_steps(x, near, far):
    lines = x.reshape(-1, *x.shape[1:][-1:])
    padded = rows_for(lines, lax.axis_size(near))
    own = lax.psum_scatter(padded, near, scatter_dimension=0, tiled=True)
    own = lax.psum(own, far)
    whole = lax.all_gather(own, near, axis=0, tiled=True)
    return whole[: len(lines)].reshape(x.shape)


def cross_product(left, right):
    return jnp.stack(
        [
            left[1] * right[2] - left[2] * right[1],
            left[2] * right[0] - left[0] * right[2],
            left[0] * right[1] - left[1] * right[0],
        ]
    )


def assemble(visible, neighbours, pair_index, pair_live):
    columns = visible.shape[2]
    frames = neighbours.shape[1]
    slots = neighbours.shape[0]
    centres = jnp.mean(visible, axis=1)
    own_frame = pair_index[0]
    slot_of = pair_index[1]
    atom_a = pair_index[2]
    atom_b = pair_index[3]
    self_column = own_frame + (columns - frames)
    partner = jnp.take(neighbours.reshape(-1), slot_of * frames + own_frame, axis=0)
    flat_coords = visible.reshape(3, -1)
    pos_a = jnp.take(flat_coords, atom_a * columns + self_column, axis=1)
    pos_b = jnp.take(flat_coords, atom_b * columns + partner, axis=1)
    arm_a = pos_a - jnp.take(centres, self_column, axis=1)
    arm_b = pos_b - jnp.take(centres, partner, axis=1)
    spring = pos_a - pos_b
    length_sq = jnp.maximum(jnp.sum(spring * spring, axis=0), 1.0)
    weight = stiffness * pair_live.astype(jnp.float32) / length_sq
    left_vec = jnp.concatenate([spring, cross_product(arm_a, spring)], axis=0)
    right_vec = jnp.concatenate([spring, cross_product(arm_b, spring)], axis=0)
    off_terms = -(weight * left_vec)[:, None, :] * right_vec[None, :, :]
    self_terms = (weight * left_vec)[:, None, :] * left_vec[None, :, :]
    values = jnp.concatenate([off_terms.reshape(36, -1).T, self_terms.reshape(36, -1).T], axis=0)
    row_keys = jnp.concatenate([slot_of * frames + own_frame, own_frame], axis=0)
    blocks = jnp.zeros((slots * frames, 36), jnp.float32).at[row_keys].add(values)
    return blocks.reshape(slots, frames, 36)


def apply_blocks(blocks, neighbours, vector_table):
    frames = neighbours.shape[1]
    vector_count = vector_table.shape[1] // 6

    def add_slot(slot_index, totals):
        gathered = jnp.take(vector_table, neighbours[slot_index], axis=0)
        coeffs = blocks[slot_index]
        pieces = [
            gathered[:, inner_dof * vector_count : (inner_dof + 1) * vector_count]
            for inner_dof in range(6)
        ]
        updated = []
        for outer_dof in range(6):
            total = totals[outer_dof]
            for inner_dof in range(6):
                column = coeffs[:, 6 * outer_dof + inner_dof : 6 * outer_dof + inner_dof + 1]
                total = total + column * pieces[inner_dof].astype(jnp.float32)
            updated.append(total)
        return tuple(updated)

    start = tuple((jnp.zeros((frames, vector_count), jnp.float32) for outer_dof in range(6)))
    totals = lax.fori_loop(0, neighbours.shape[0], add_slot, start)
    return jnp.concatenate(totals, axis=1)


def gram_matrix(left, right):
    return lax.dot_general(
        left, right, (((0,), (0,)), ((), ())), preferred_element_type=jnp.float32
    )


def rayleigh_ritz(basis_gram, cross_gram, image_gram, image_rows, total_rows):
    factor = jnp.linalg.cholesky(basis_gram / total_rows)
    sym_cross = (cross_gram + cross_gram.T) / (2.0 * total_rows)
    half_solved = lax.linalg.triangular_solve(factor, sym_cross, left_side=True, lower=True)
    ritz_matrix = lax.linalg.triangular_solve(factor, half_solved.T, left_side=True, lower=True)
    image_factor = jnp.linalg.cholesky(image_gram / total_rows)
    next_rows = lax.linalg.triangular_solve(
        image_factor, image_rows, left_side=False, lower=True, transpose_a=True
    )
    return (ritz_matrix, next_rows)


def per_device(coordinates, neighbours, pair_index, pair_live, basis):
    frames = basis.shape[3]
    vector_count = basis.shape[4] // 6
    rim_frames = frames // 4
    atoms_per = coordinates.shape[4]
    total_rows = 6 * frames * lax.axis_size(GX) * lax.axis_size("gy") * lax.axis_size(GZ)
    own_basis = basis[0, 0, 0]
    own_lists = neighbours[0, 0, 0]
    flat_basis = own_basis.reshape(frames * 6, vector_count)
    basis_local = gram_matrix(flat_basis, flat_basis)
    near_coords = padded(
        coordinates[:, :, :, :, :, :rim_frames], ((GX, 0), ("gy", 1), (GZ, 2)), 1, False
    )
    rim_rows = basis[:, :, :, :rim_frames, :]
    near_basis = padded(rim_rows, ((GX, 0), ("gy", 1), (GZ, 2)), 1, False)
    ghost_coords = (
        near_coords.reshape(27, 3, atoms_per, rim_frames)
        .transpose(1, 2, 0, 3)
        .reshape(3, atoms_per, 27 * rim_frames)
    )
    visible = jnp.concatenate([ghost_coords, coordinates[0, 0, 0]], axis=2)
    blocks = assemble(visible, own_lists, pair_index[0, 0, 0], pair_live[0, 0, 0])
    vector_table = jnp.concatenate(
        [near_basis.reshape(27 * rim_frames, 6 * vector_count), own_basis], axis=0
    )
    image_rows = apply_blocks(blocks, own_lists, vector_table)
    rounded = image_rows.astype(jnp.bfloat16).reshape(frames * 6, vector_count)
    cross_local = gram_matrix(flat_basis, rounded)
    image_local = gram_matrix(rounded, rounded)
    basis_gram, cross_gram, image_gram = (
        sum_in_two_steps(basis_local, "gz_1", ("gx_0", "gx_1", "gy", "gz_0")),
        sum_in_two_steps(cross_local, "gz_1", ("gx_0", "gx_1", "gy", "gz_0")),
        sum_in_two_steps(image_local, "gz_1", ("gx_0", "gx_1", "gy", "gz_0")),
    )
    ritz_matrix, next_rows = rayleigh_ritz(
        basis_gram, cross_gram, image_gram, image_rows.reshape(frames * 6, vector_count), total_rows
    )
    next_basis = next_rows.reshape(1, 1, 1, frames, 6 * vector_count)
    return (next_basis, ritz_matrix)


def solution(mesh):
    torus = Mesh(
        mesh.devices.reshape(2, 4, mesh.shape["gy"], 4, 2), ("gx_0", "gx_1", "gy", "gz_0", "gz_1")
    )
    in_specs = (
        P(GX, "gy", GZ, None, None, None),
        P(GX, "gy", GZ, None, None),
        P(GX, "gy", GZ, None, None),
        P(GX, "gy", GZ, None),
        P(GX, "gy", GZ, None, None),
    )
    out_specs = (P(GX, "gy", GZ, None, None), P())
    return jax.shard_map(
        per_device, mesh=torus, in_specs=in_specs, out_specs=out_specs, check_vma=False
    )
```

profile of v0, /device:TPU:1, one launch (start us, length us, event | category | flops | bytes accessed | tf_op | source)
XLA Modules:
  0.0 1204.1 jit_solution(14516050575677457552)
XLA Ops:
  7.2 4.0 collective-permute-start
  13.5 4.0 collective-permute-start.6
  24.2 84.9 %gather_fusion.1 = s32[15360]{0:T(1024)S(1)} fusion(s32[2048]{0:T(1024)S(1)} %bitcast.221, s32[15360]{0:T(1024)S(1)} %broadcast_clamp_fusion), kind=kCustom, calls=%fused_computation.5 | custom fusion | bytes 184320 | tf_op jit(solution)/shard_map/jit(_take)/gather | solution.py:65
  118.4 7.7 collective-permute-start.4
  129.0 5.3 collective-permute-done.5
  134.9 4.6 copy.145
  139.6 54.4 %gather_fusion.3 = f32[15360,3]{1,0:T(8,128)} fusion(f32[3,15872]{0,1:T(8,128)} %bitcast.223, s32[15360]{0:T(1024)S(1)} %get-tuple-element.414), kind=kCustom, calls=%fused_computation.3.clone | custom fusion | bytes 430080 | tf_op jit(solution)/shard_map/jit(_take)/gather | solution.py:68
  194.0 5.0 copy.147
  199.3 51.1 %gather_fusion.5 = f32[15360,3]{1,0:T(8,128)} fusion(f32[3,992]{0,1:T(8,128)S(1)} %broadcast_multiply_fusion.2, s32[15360]{0:T(1024)S(1)} %get-tuple-element.413), kind=kCustom, calls=%fused_computation.4.clone | custom fusion | bytes 430080 | tf_op jit(solution)/shard_map/jit(_take)/gather | solution.py:70
  250.4 5.0 copy.150
  255.4 54.4 %gather_fusion.2 = f32[15360,3]{1,0:T(8,128)} fusion(f32[3,15872]{0,1:T(8,128)} %bitcast.224, s32[15360]{0:T(1024)S(1)} %get-tuple-element.418), kind=kCustom, calls=%fused_computation.clone | custom fusion | bytes 430080 | tf_op jit(solution)/shard_map/jit(_take)/gather | solution.py:67
  309.9 5.0 copy.146
  314.9 51.1 %gather_fusion.4 = f32[15360,3]{1,0:T(8,128)} fusion(f32[3,992]{0,1:T(8,128)S(1)} %broadcast_multiply_fusion.2, s32[15360]{0:T(1024)S(1)} %get-tuple-element.417), kind=kCustom, calls=%fused_computation.1.clone | custom fusion | bytes 430080 | tf_op jit(solution)/shard_map/jit(_take)/gather | solution.py:69
  366.1 5.0 copy.149
  392.6 4.2 pad_maximum_fusion
  396.8 10.4 copy.151
  407.2 163.6 %scatter_custom_fusion = f32[2048,36]{1,0:T(8,128)S(1)} fusion(s32[30720]{0:T(1024)} %bitcast.248, f32[30720,36]{1,0:T(8,128)} %copy.151, f32[]{:T(128)} %constant.163.clone.1), kind=kCustom, calls=%fused_computation.145 | custom fusion | flops 1105920 | bytes 295424 | tf_op jit(solution)/shard_map/scatter-add | solution.py:80
  573.9 217.5 %while.30 = (s32[]{:T(128)}, f32[128,256]{1,0:T(8,128)}, f32[128,256]{1,0:T(8,128)}, f32[128,256]{1,0:T(8,128)}, f32[128,256]{1,0:T(8,128)}, /*index=5*/f32[128,...) while((s32[]{:T(128)}, f32[128,256]{1,0:T(8,128)}, ...), condition=%wide.region_4.7_spmd.clone, body=%wide.region_3.6_spmd.clone.sunk | while | flops 3934339 | bytes 5604240 | solution.py:105
  799.6 21.3 %reduce-scatter.8.cloned.1.call-done = f32[128,256]{0,1:T(8,128)} async-done(((f32[256,256]{0,1:T(8,128)}), f32[128,256]{0,1:T(8,128)}) %reduce-scatter.8.cloned.1.call-update) | async-done | bytes 131088 | tf_op jit(solution)/shard_map/reduce_scatter | solution.py:39
  820.9 17.4 %reduce-scatter.4.cloned.1.call-done = f32[128,256]{0,1:T(8,128)} async-done(((f32[256,256]{0,1:T(8,128)}), f32[128,256]{0,1:T(8,128)}) %reduce-scatter.4.cloned.1.call-update) | async-done | bytes 131088 | tf_op jit(solution)/shard_map/reduce_scatter | solution.py:39
  838.5 219.6 %all-reduce.4.cloned.1.call-done = (f32[128,256]{0,1:T(8,128)}, f32[128,256]{0,1:T(8,128)}, f32[128,256]{0,1:T(8,128)}) async-done(((f32[128,256]{0,1:T(8,128)}, f32[128,256]{0,1:T(8,128)}, f32[128,256]{0,1:T(8,128)}), (f32[128,256]{0,1:T(8,128)}, f32[128,256]{0,1:T(8,128)}, f32[128,256]{0,1:T(8,128)})) %all-reduce.4.cloned.1.call-update) | async-done | bytes 393232 | tf_op jit(solution)/shard_map/psum | solution.py:40
  1058.0 7.6 all_gather.10
  1065.8 11.7 cholesky.164
  1077.6 9.8 custom-call.24
  1087.9 11.7 cholesky.181
  1102.5 4.3 while.31
  1106.8 19.7 %custom-call.26 = f32[2,128,128]{1,2,0:T(8,128)S(1)} custom-call(f32[2,128,128]{2,1,0:T(8,128)S(1)} %get-tuple-element.242), custom_call_target="InvertDiagBlocksLowerTriangular" | custom-call | tf_op jit(solution)/shard_map/triangular_solve/custom-call.4 | solution.py:119
  1133.7 11.7 cholesky.130
  1145.5 9.8 custom-call.23
  1155.8 11.7 cholesky.147
  1170.2 4.2 while.29
  1174.3 19.7 %custom-call.14 = f32[2,128,128]{1,2,0:T(8,128)S(1)} custom-call(f32[2,128,128]{2,1,0:T(8,128)S(1)} %get-tuple-element.201), custom_call_target="InvertDiagBlocksLowerTriangular" | custom-call | tf_op jit(solution)/shard_map/triangular_solve | solution.py:121
  (386 shorter events, 294.1 us)
Async XLA Ops:
  7.2 17.0 %copy-start.11 = (s32[1,1,1,15360]{3,2,1,0:T(1,128)S(1)}, s32[1,1,1,15360]{3,2,1,0:T(1,128)}, u32[]{:S(2)}) copy-start(s32[1,1,1,15360]{3,2,1,0:T(1,128)} %param.17) | copy-start | bytes 184324
  7.2 17.0 %copy-start = (s32[1,1,1,16,128]{4,3,2,1,0:T(8,128)S(1)}, s32[1,1,1,16,128]{4,3,2,1,0:T(8,128)}, u32[]{:S(2)}) copy-start(s32[1,1,1,16,128]{4,3,2,1,0:T(8,128)} %param.15) | copy-start | bytes 24580
  7.2 792.4 %reduce-scatter.6.cloned.1.call-start = ((), (), s32[]{:S(2)}) async-start(), calls=%async_computation.4 | async-start | bytes 393216 | tf_op jit(solution)/shard_map/reduce_scatter | solution.py:39
  7.2 102.8 %collective-permute-start = (f32[1,1,1,3,16,32]{5,4,3,2,1,0:T(8,128)}, f32[1,1,1,3,16,32]{5,4,3,2,1,0:T(8,128)S(1)}, u32[]{:S(2)}, u32[]{:S(2)}) collective-permute-start(f32[1,1,1,3,16,32]{5,4,3,2,1,0:T(8,128)} %bitcast.240), channel_id=1, source_target_pairs={{0,32},{32,64},{64,96},{96,128},{128,160},{160,192},{192,224},{1,3... | collective-permute-start | bytes 18440 | tf_op jit(solution)/shard_map/ppermute | solution.py:22
  11.3 98.8 %collective-permute-start.1 = (f32[1,1,1,3,16,32]{5,4,3,2,1,0:T(8,128)}, f32[1,1,1,3,16,32]{5,4,3,2,1,0:T(8,128)S(1)}, u32[]{:S(2)}, u32[]{:S(2)}) collective-permute-start(f32[1,1,1,3,16,32]{5,4,3,2,1,0:T(8,128)} %bitcast.241), channel_id=1, source_target_pairs={{32,0},{64,32},{96,64},{128,96},{160,128},{192,160},{224,192},{33,... | collective-permute-start | bytes 18440 | tf_op jit(solution)/shard_map/ppermute | solution.py:24
  13.5 359.4 %collective-permute-start.6 = (bf16[1,1,1,32,1536]{4,3,2,1,0:T(8,128)(2,1)S(1)}, bf16[1,1,1,32,1536]{4,3,2,1,0:T(8,128)(2,1)S(1)}, u32[]{:S(2)}, u32[]{:S(2)}) collective-permute-start(bf16[1,1,1,32,1536]{4,3,2,1,0:T(8,128)(2,1)S(1)} %slice.420), channel_id=1, source_target_pairs={{0,32},{32,64},{64,96},{96,128},{128,160},{160,192},{192,224},{1,3... | collective-permute-start | bytes 294920 | tf_op jit(solution)/shard_map/ppermute | solution.py:22
  17.5 355.4 %collective-permute-start.7 = (bf16[1,1,1,32,1536]{4,3,2,1,0:T(8,128)(2,1)S(1)}, bf16[1,1,1,32,1536]{4,3,2,1,0:T(8,128)(2,1)S(1)}, u32[]{:S(2)}, u32[]{:S(2)}) collective-permute-start(bf16[1,1,1,32,1536]{4,3,2,1,0:T(8,128)(2,1)S(1)} %slice.420), channel_id=1, source_target_pairs={{32,0},{64,32},{96,64},{128,96},{160,128},{192,160},{224,192},{33,... | collective-permute-start | bytes 294920 | tf_op jit(solution)/shard_map/ppermute | solution.py:24
  20.1 89.1 %copy-start.2 = (bf16[768,256]{1,0:T(8,128)(2,1)}, bf16[768,256]{1,0:T(8,128)(2,1)S(1)}, u32[]{:S(2)}) copy-start(bf16[768,256]{1,0:T(8,128)(2,1)S(1)} %reshape_squeeze.7) | copy-start | bytes 1179652
  21.1 799.7 %reduce-scatter.8.cloned.1.call-start = ((), (), s32[]{:S(2)}) async-start(), calls=%async_computation.5 | async-start | bytes 393216 | tf_op jit(solution)/shard_map/reduce_scatter | solution.py:39
  24.2 85.9 %copy-start.8 = (f32[1,1,1,3,16,128]{5,4,3,2,1,0:T(8,128)S(1)}, f32[1,1,1,3,16,128]{5,4,3,2,1,0:T(8,128)}, u32[]{:S(2)}) copy-start(f32[1,1,1,3,16,128]{5,4,3,2,1,0:T(8,128)} %param.14) | copy-start | bytes 73732
  110.1 4.5 collective-permute-start.2
  113.2 5.1 collective-permute-start.3
  118.4 10.6 collective-permute-start.4
  126.1 8.2 collective-permute-start.5
  372.9 12.2 %copy-start.6 = (bf16[1,1,1,32,1536]{4,3,2,1,0:T(8,128)(2,1)}, bf16[1,1,1,32,1536]{4,3,2,1,0:T(8,128)(2,1)S(1)}, u32[]{:S(2)}) copy-start(bf16[1,1,1,32,1536]{4,3,2,1,0:T(8,128)(2,1)S(1)} %collective-permute-done.7) | copy-start | bytes 294916
  373.6 11.4 collective-permute-start.8
  376.8 8.3 collective-permute-start.9
  381.6 11.0 copy-start.1
  385.0 11.8 copy-start.5
  387.2 184.7 %collective-permute-start.10 = (bf16[3,3,1,32,1536]{4,3,2,1,0:T(8,128)(2,1)}, bf16[3,3,1,32,1536]{4,3,2,1,0:T(8,128)(2,1)}, u32[]{:S(2)}, u32[]{:S(2)}) collective-permute-start(bf16[3,3,1,32,1536]{4,3,2,1,0:T(8,128)(2,1)} %pad_maximum_fusion.3), channel_id=1, source_target_pairs={{0,1},{1,2},{2,3},{3,4},{4,5},{5,6},{6,7},{8,9},{9,10},{10,11},{11... | collective-permute-start | bytes 2654216 | tf_op jit(solution)/shard_map/ppermute | solution.py:22
  389.7 182.2 %collective-permute-start.11 = (bf16[3,3,1,32,1536]{4,3,2,1,0:T(8,128)(2,1)}, bf16[3,3,1,32,1536]{4,3,2,1,0:T(8,128)(2,1)}, u32[]{:S(2)}, u32[]{:S(2)}) collective-permute-start(bf16[3,3,1,32,1536]{4,3,2,1,0:T(8,128)(2,1)} %pad_maximum_fusion.3), channel_id=1, source_target_pairs={{1,0},{2,1},{3,2},{4,3},{5,4},{6,5},{7,6},{9,8},{10,9},{11,10},{12... | collective-permute-start | bytes 2654216 | tf_op jit(solution)/shard_map/ppermute | solution.py:24
  396.8 175.1 %copy-start.7 = (bf16[1,1,1,32,1536]{4,3,2,1,0:T(8,128)(2,1)S(1)}, bf16[1,1,1,32,1536]{4,3,2,1,0:T(8,128)(2,1)}, u32[]{:S(2)}) copy-start(bf16[1,1,1,32,1536]{4,3,2,1,0:T(8,128)(2,1)} %copy-done.6) | copy-start | bytes 294916
  570.8 2.9 copy-start.4
  791.4 6.0 copy-start.3
  798.4 39.8 %reduce-scatter.4.cloned.1.call-start = ((), (), s32[]{:S(2)}) async-start(), calls=%async_computation.3 | async-start | bytes 393216 | tf_op jit(solution)/shard_map/reduce_scatter | solution.py:39
  799.5 258.5 %all-reduce.4.cloned.1.call-start = ((), (), s32[]{:S(2)}) async-start(), calls=%async_computation.6 | async-start | bytes 786432 | tf_op jit(solution)/shard_map/psum | solution.py:40
  1058.0 68.4 %copy-start.10 = (f32[128,256]{0,1:T(8,128)S(1)}, f32[128,256]{0,1:T(8,128)}, u32[]{:S(2)}) copy-start(f32[128,256]{0,1:T(8,128)} %get-tuple-element.340) | copy-start | bytes 393220
  1102.4 29.1 %copy-start.9 = (f32[128,256]{0,1:T(8,128)S(1)}, f32[128,256]{0,1:T(8,128)}, u32[]{:S(2)}) copy-start(f32[128,256]{0,1:T(8,128)} %get-tuple-element.339) | copy-start | bytes 393220
Sparse Core Ops, SparseCore 0:
  21.3 19.8 reduce-scatter.5
  798.5 22.2 reduce-scatter.7
  823.9 14.3 reduce-scatter.3
  843.9 214.1 all-reduce.3
where the time goes:
time: 1220 us; the launch traced here: 1200 us
  other arithmetic  469 us (38%)
  local copies, waits for them, and re-layouts  394 us (32%)
  waiting for transfers between devices  268 us (22%)
  starting transfers between devices  34.7 us (3%)
  between operations  17.4 us (1%)
    psum x1, waiting for transfers between devices, sum_in_two_steps(): own = lax.psum(own, far)  220 us
    scatter-add x1, other arithmetic, assemble(): jnp.zeros((slots * frames, 36), jnp.float32).at[row_keys].add(values)  164 us
    add x96, other arithmetic, add_slot(): total = total + column * pieces[inner_dof].astype(jnp.float32)  161 us
    gather x1, local copies, waits for them, and re-layouts, assemble(): jnp.take(neighbours.reshape(-1), slot_of * frames + own_frame, axis=0)  84.9 us
    gather x2, local copies, waits for them, and re-layouts, assemble(): pos_a = jnp.take(flat_coords, atom_a * columns + self_column, axis=1)  59.5 us
    gather x2, local copies, waits for them, and re-layouts, assemble(): pos_b = jnp.take(flat_coords, atom_b * columns + partner, axis=1)  59.4 us
    gather x2, local copies, waits for them, and re-layouts, assemble(): arm_a = pos_a - jnp.take(centres, self_column, axis=1)  56.2 us
    gather x2, local copies, waits for them, and re-layouts, assemble(): arm_b = pos_b - jnp.take(centres, partner, axis=1)  56.2 us
  transfers between devices with their start and end apart: 16, of which 6 were waited for; matrix products, arithmetic and copies ran while one was open for 62% of the time, Pallas kernels for 0%

commit v1 on v0

v1 whole, which is shorter than its diff:
```python
import functools
import jax
import jax.numpy as jnp
from jax import lax
from jax.experimental import pallas as pl
from jax.experimental.pallas import tpu as pltpu
from jax.sharding import PartitionSpec as P

VM = pl.BlockSpec(memory_space=pltpu.VMEM)
BIG = 60 * 1024 * 1024
F = 128
K = 256
NB = 16
PB = 4096.0
CHUNK = 3840
STEP = 768


def count_body(pairs_ref, live_ref, hist_ref, acc_ref):
    rows = lax.broadcasted_iota(jnp.int32, (256, STEP), 0)
    zero = jnp.zeros((256, STEP), jnp.float32)

    def chunk(c, first):
        def step(t, carry):
            at = pl.ds(pl.multiple_of(c * CHUNK + t * STEP, 128), STEP)
            f = pairs_ref[0:1, at]
            s = pairs_ref[1:2, at]
            a = pairs_ref[2:3, at]
            b = pairs_ref[3:4, at]
            live = live_ref[0:1, at]
            value = (live * jnp.where(a >= 8, int(PB), 1)).astype(jnp.float32)
            col = ((a >> 2) & 1) * 128 + f
            right = jnp.where(rows == col, jnp.broadcast_to(value, (256, STEP)), zero).astype(jnp.bfloat16)
            hot = rows == (b * 16 + s)
            low = a & 3
            for part in range(4):
                mark = jnp.broadcast_to((low == part).astype(jnp.float32), (256, STEP))
                left = jnp.where(hot, mark, zero).astype(jnp.bfloat16)
                got = lax.dot_general(left, right, (((1,), (1,)), ((), ())), preferred_element_type=jnp.float32)
                here = pl.ds(part * 256, 256)
                acc_ref[here, :] = acc_ref[here, :] + got
            return carry

        acc_ref[...] = jnp.zeros_like(acc_ref)
        lax.fori_loop(0, CHUNK // STEP, step, 0)
        for part in range(4):
            got = acc_ref[part * 256 : (part + 1) * 256, :]
            high = jnp.floor(got * (1.0 / PB))
            lower = got - PB * high
            for mid in range(2):
                lanes = slice(mid * 128, (mid + 1) * 128)
                for top, val in ((0, lower), (1, high)):
                    a = top * 8 + mid * 4 + part
                    here = slice(a * 256, (a + 1) * 256)
                    if first:
                        hist_ref[here, :] = val[:, lanes]
                    else:
                        hist_ref[here, :] = hist_ref[here, :] + val[:, lanes]

    chunk(0, True)

    def more(c, carry):
        chunk(c, False)
        return carry

    lax.fori_loop(1, pairs_ref.shape[1] // CHUNK, more, 0)


def count_pairs(pairs, live):
    return pl.pallas_call(
        count_body,
        out_shape=jax.ShapeDtypeStruct((4096, 128), jnp.float32),
        in_specs=[VM, VM],
        out_specs=VM,
        scratch_shapes=[pltpu.VMEM((1024, 256), jnp.float32)],
        compiler_params=pltpu.CompilerParams(vmem_limit_bytes=BIG),
        cost_estimate=pl.CostEstimate(flops=8 * 10**9, bytes_accessed=3 * 10**6, transcendentals=0),
        name="count_pairs",
    )(pairs, live)


def cross(p, q):
    return [
        p[1] * q[2] - p[2] * q[1],
        p[2] * q[0] - p[0] * q[2],
        p[0] * q[1] - p[1] * q[0],
    ]


SYM = ((0, 0), (0, 1), (0, 2), (1, 1), (1, 2), (2, 2))


def symmetric(six):
    return [[six[0], six[1], six[2]], [six[1], six[3], six[4]], [six[2], six[4], six[5]]]


def moments(hist_ref, coords_ref, q_ref, blk_ref, rr_ref):
    blk_ref[...] = jnp.zeros_like(blk_ref)
    rr_ref[...] = jnp.zeros_like(rr_ref)
    own = [jnp.sum(coords_ref[16 * c : 16 * c + 16, :], axis=0, keepdims=True) * (1.0 / 16.0) for c in range(3)]
    for half in range(2):
        def tile(c, b):
            return q_ref[(c * 16 + b) * 16 + half * 8 : (c * 16 + b) * 16 + half * 8 + 8, :]

        centre = []
        for c in range(3):
            total = tile(c, 0)
            for b in range(1, 16):
                total = total + tile(c, b)
            centre.append(total * (1.0 / 16.0))

        def atom(a, carry):
            r = [jnp.broadcast_to(coords_ref[pl.ds(c * 16 + a, 1), :], (8, F)) for c in range(3)]
            arm = [r[c] - jnp.broadcast_to(own[c], (8, F)) for c in range(3)]
            m = [None] * 6
            n = [[None] * 3 for _ in range(3)]
            for b in range(16):
                q = [tile(c, b) for c in range(3)]
                d = [r[c] - q[c] for c in range(3)]
                count = hist_ref[pl.ds(pl.multiple_of(a * 256 + b * 16 + half * 8, 8), 8), :]
                w = (0.01 * count) / jnp.maximum(d[0] * d[0] + d[1] * d[1] + d[2] * d[2], 1.0)
                wd = [w * d[c] for c in range(3)]
                turn = cross([q[c] - centre[c] for c in range(3)], d)
                for k, (j, i) in enumerate(SYM):
                    t = wd[j] * d[i]
                    m[k] = t if m[k] is None else m[k] + t
                for j in range(3):
                    for i in range(3):
                        t = wd[j] * turn[i]
                        n[j][i] = t if n[j][i] is None else n[j][i] + t
            m = symmetric(m)
            rt = [cross(arm, [m[j][i] for j in range(3)]) for i in range(3)]
            rn = [cross(arm, [n[j][i] for j in range(3)]) for i in range(3)]
            for j in range(3):
                for i in range(3):
                    for jj, ii, val in ((j, i, m[j][i]), (j, 3 + i, n[j][i]), (3 + j, i, rt[i][j]), (3 + j, 3 + i, rn[i][j])):
                        here = pl.ds((jj * 6 + ii) * 16 + half * 8, 8)
                        blk_ref[here, :] = blk_ref[here, :] - val
            for j in range(3):
                rr = cross(arm, [rt[i][j] for i in range(3)])
                for i in range(3):
                    here = pl.ds((j * 3 + i) * 8, 8)
                    rr_ref[here, :] = rr_ref[here, :] + rr[i]
            return carry

        lax.fori_loop(0, 16, atom, 0)
    for j in range(3):
        for i in range(3):
            tt = jnp.sum(blk_ref[pl.ds((j * 6 + i) * 16, 16), :], axis=0, keepdims=True)
            rt = jnp.sum(blk_ref[pl.ds(((3 + j) * 6 + i) * 16, 16), :], axis=0, keepdims=True)
            rr = jnp.sum(rr_ref[pl.ds((j * 3 + i) * 8, 8), :], axis=0, keepdims=True)
            for jj, ii, val in ((j, i, -tt), (3 + j, i, -rt), (i, 3 + j, -rt), (3 + j, 3 + i, rr)):
                here = pl.ds((jj * 6 + ii) * 16, 1)
                rr_ref[72 + jj * 6 + ii : 73 + jj * 6 + ii, :] = val
    for ji in range(36):
        here = pl.ds(ji * 16, 1)
        blk_ref[here, :] = blk_ref[here, :] + rr_ref[72 + ji : 73 + ji, :]


KC = 32


def apply_body(hist_ref, table_ref, lists_ref, coords_ref, image_ref, gram_ref, hot_ref, q_ref, g_ref, blk_ref, rr_ref, it_ref, x_ref, y_ref):
    cols = table_ref.shape[0]
    for s in range(NB):
        near = jnp.broadcast_to(lists_ref[s : s + 1, :], (cols, F))
        hot = lax.broadcasted_iota(jnp.int32, (cols, F), 0) == near
        hot_ref[:, s * F : (s + 1) * F] = jnp.where(hot, 1.0, 0.0).astype(jnp.bfloat16)

    def gather(lo, hi):
        return lax.dot_general(table_ref[:, lo:hi], hot_ref[...], (((0,), (0,)), ((), ())), preferred_element_type=jnp.float32)

    got = gather(6 * K, 6 * K + 256)
    pos = got[0:48] + got[48:96] + got[96:144]
    for s in range(NB):
        for t in range(6):
            q_ref[pl.ds(t * 128 + s, 8, stride=16), :] = pos[t * 8 : t * 8 + 8, s * F : (s + 1) * F]
    moments(hist_ref, coords_ref, q_ref, blk_ref, rr_ref)
    for i in range(6):
        g_ref[i * K : (i + 1) * K, :] = gather(i * K, (i + 1) * K)

    def piece(kc, carry):
        start = pl.multiple_of(kc * KC, KC)
        totals = [jnp.zeros((KC, F), jnp.float32) for _ in range(6)]
        for s in range(NB):
            for i in range(6):
                g = g_ref[pl.ds(i * K + start, KC), s * F : (s + 1) * F]
                for j in range(6):
                    row = (j * 6 + i) * 16 + s
                    totals[j] = totals[j] + jnp.broadcast_to(blk_ref[row : row + 1, :], (KC, F)) * g
        for j in range(6):
            it_ref[pl.ds(j * K + start, KC), :] = totals[j]
        return carry

    lax.fori_loop(0, K // KC, piece, 0)
    own = cols - F
    for j in range(6):
        y = jnp.transpose(it_ref[j * K : (j + 1) * K, :])
        image_ref[j * F : (j + 1) * F, :] = y
        y_ref[j * F : (j + 1) * F, :] = y.astype(jnp.bfloat16)
        x_ref[j * F : (j + 1) * F, :] = table_ref[own:cols, j * K : (j + 1) * K]
    for n, (p, q) in enumerate(((x_ref, x_ref), (x_ref, y_ref), (y_ref, y_ref))):
        gram = lax.dot_general(p[...], q[...], (((0,), (0,)), ((), ())), preferred_element_type=jnp.float32)
        gram_ref[n * K : (n + 1) * K, :] = gram


def apply_pairs(hist, table, lists, coords):
    cols = table.shape[0]
    return pl.pallas_call(
        apply_body,
        out_shape=(jax.ShapeDtypeStruct((6 * F, K), jnp.float32), jax.ShapeDtypeStruct((3 * K, K), jnp.float32)),
        in_specs=[VM] * 4,
        out_specs=(VM, VM),
        scratch_shapes=[
            pltpu.VMEM((cols, NB * F), jnp.bfloat16),
            pltpu.VMEM((768, F), jnp.float32),
            pltpu.VMEM((6 * K, NB * F), jnp.float32),
            pltpu.VMEM((576, F), jnp.float32),
            pltpu.VMEM((112, F), jnp.float32),
            pltpu.VMEM((6 * K, F), jnp.float32),
            pltpu.VMEM((6 * F, K), jnp.bfloat16),
            pltpu.VMEM((6 * F, K), jnp.bfloat16),
        ],
        compiler_params=pltpu.CompilerParams(vmem_limit_bytes=BIG),
        cost_estimate=pl.CostEstimate(flops=8 * 10**9, bytes_accessed=8 * 10**6, transcendentals=0),
        name="apply_pairs",
    )(hist, table, lists, coords)


def three_parts(rows):
    def cut(x):
        return lax.reduce_precision(x, 8, 7)

    high = cut(rows)
    mid = cut(rows - high)
    low = rows - high - mid
    return jnp.concatenate([high.astype(jnp.bfloat16), mid.astype(jnp.bfloat16), low.astype(jnp.bfloat16)], axis=1)


def extended(basis, coords):
    frames = basis.shape[0]
    flat = coords.reshape(48, frames).T
    parts = three_parts(flat)
    return jnp.concatenate([basis, parts, jnp.zeros((frames, 256 - 144), jnp.bfloat16)], axis=1)

MESH = pl.DeviceIdType.MESH


def place():
    gx, gy, gz = lax.axis_index("gx"), lax.axis_index("gy"), lax.axis_index("gz")
    y, z = lax.rem(gx, 4), lax.div(gz, 2) * 2 + lax.div(gx, 4)
    return gy, y, z, lax.rem(gz, 2)


def device(x, y, z, core):
    return {"gx": lax.rem(z, 2) * 4 + y, "gy": x, "gz": lax.div(z, 2) * 2 + core}


def total_body(gram_ref, out_ref, tail_ref, data, half_in, half, y_in, part, x_in, z_in, t1, t2, t3, t4, send, recv):
    x, y, z, core = place()
    across = [device(x, y, z, 1 - core)]
    along_y = [device(x, lax.rem(y + d, 4), z, core) for d in range(1, 4)]
    along_x = [device(lax.rem(x + d, 4), y, z, core) for d in range(1, 4)]
    along_z = [device(x, y, lax.rem(z + d, 8), core) for d in range(1, 8)]
    barrier = pltpu.get_barrier_semaphore()
    for peer in across + along_y + along_x + along_z:
        pl.semaphore_signal(barrier, inc=1, device_id=peer, device_id_type=MESH)

    lower = lax.broadcasted_iota(jnp.int32, (F, F), 0) >= lax.broadcasted_iota(jnp.int32, (F, F), 1)
    eye = lax.broadcasted_iota(jnp.int32, (F, F), 0) == lax.broadcasted_iota(jnp.int32, (F, F), 1)
    t1[0] = jnp.zeros((8, F), jnp.float32)
    for m in range(3):
        b11 = gram_ref[m * K : m * K + F, 0:F]
        b21 = gram_ref[m * K + F : m * K + K, 0:F]
        b22 = gram_ref[m * K + F : m * K + K, F:K]
        if m == 1:
            b11 = b11 + b11.T
            b21 = b21 + gram_ref[m * K : m * K + F, F:K].T
            b22 = b22 + b22.T
        data[m * 32 : m * 32 + 16] = b21.reshape(16, 8, F)
        data[m * 32 + 16 : m * 32 + 32] = jnp.where(lower, b11, b22).reshape(16, 8, F)
        t1[0, m : m + 1, :] = jnp.sum(jnp.where(eye, b22, 0.0), axis=0, keepdims=True)
    pl.semaphore_wait(barrier, 14)

    count = [0]

    def copy(src, dst, peer):
        n = count[0]
        count[0] += 1
        return pltpu.make_async_remote_copy(src_ref=src, dst_ref=dst, send_sem=send.at[n], recv_sem=recv.at[n], device_id=peer, device_id_type=MESH)

    def run(copies):
        for c in copies:
            c.start()
        for c in copies:
            c.wait()

    run([
        copy(data.at[pl.ds((1 - core) * 48, 48)], half_in, across[0]),
        copy(t1.at[0], t1.at[1], across[0]),
    ])
    half[...] = data[pl.ds(core * 48, 48)] + half_in[...]
    t2[y] = t1[0] + t1[1]
    run(
        [copy(half.at[pl.ds(lax.rem(y + d, 4) * 12, 12)], y_in.at[d - 1], along_y[d - 1]) for d in range(1, 4)]
        + [copy(t2.at[y], t2.at[y], along_y[d - 1]) for d in range(1, 4)]
    )
    part[...] = half[pl.ds(y * 12, 12)] + y_in[0] + y_in[1] + y_in[2]
    t3[x] = t2[0] + t2[1] + t2[2] + t2[3]
    run(
        [copy(part.at[pl.ds(lax.rem(x + d, 4) * 3, 3)], x_in.at[d - 1], along_x[d - 1]) for d in range(1, 4)]
        + [copy(t3.at[x], t3.at[x], along_x[d - 1]) for d in range(1, 4)]
    )
    z_in[z] = part[pl.ds(x * 3, 3)] + x_in[0] + x_in[1] + x_in[2]
    t4[z] = t3[0] + t3[1] + t3[2] + t3[3]
    run(
        [copy(z_in.at[z], z_in.at[z], along_z[d - 1]) for d in range(1, 8)]
        + [copy(t4.at[z], t4.at[z], along_z[d - 1]) for d in range(1, 8)]
    )
    total, tail = z_in[0], t4[0]
    for n in range(1, 8):
        total = total + z_in[n]
        tail = tail + t4[n]
    tail_ref[...] = tail
    mine = core * 48 + y * 12 + x * 3
    out_ref[pl.ds(mine, 3)] = total
    run([copy(out_ref.at[pl.ds(mine, 3)], out_ref.at[pl.ds(mine, 3)], along_x[d - 1]) for d in range(1, 4)])
    mine = core * 48 + y * 12
    run([copy(out_ref.at[pl.ds(mine, 12)], out_ref.at[pl.ds(mine, 12)], along_y[d - 1]) for d in range(1, 4)])
    mine = core * 48
    run([copy(out_ref.at[pl.ds(mine, 48)], out_ref.at[pl.ds(mine, 48)], across[0])])


def total_grams(gram):
    def buf(*shape):
        return pltpu.VMEM((*shape, 8, F), jnp.float32)

    return pl.pallas_call(
        total_body,
        out_shape=(jax.ShapeDtypeStruct((96, 8, F), jnp.float32), jax.ShapeDtypeStruct((8, F), jnp.float32)),
        in_specs=[VM],
        out_specs=(VM, VM),
        scratch_shapes=[
            buf(96), buf(48), buf(48), buf(3, 12), buf(12), buf(3, 3), buf(8, 3), buf(2), buf(4), buf(4), buf(8),
            pltpu.SemaphoreType.DMA((35,)), pltpu.SemaphoreType.DMA((35,)),
        ],
        compiler_params=pltpu.CompilerParams(collective_id=1, has_side_effects=True, vmem_limit_bytes=16 * 1024 * 1024),
        cost_estimate=pl.CostEstimate(flops=10**6, bytes_accessed=2 * 10**6, transcendentals=0),
        name="total_grams",
    )(gram)


def dot32(p, q, dims):
    return lax.dot_general(p, q, (dims, ((), ())), precision=lax.Precision.HIGHEST, preferred_element_type=jnp.float32)


NT = ((1,), (1,))
NN = ((1,), (0,))


def eliminate(mats):
    sub = lax.broadcasted_iota(jnp.int32, (8, F), 0)
    lane = lax.broadcasted_iota(jnp.int32, (8, F), 1)
    tiles = [[m[8 * t : 8 * t + 8, :] for t in range(16)] for m in mats]
    for j in range(F):
        t, r = divmod(j, 8)
        at = lane == j
        for rows in tiles:
            pivot = rows[t]
            inv = 1.0 / jnp.broadcast_to(pivot[r : r + 1, j : j + 1], (8, F))
            scaled = jnp.where(at, 1.0, jnp.broadcast_to(pivot[r : r + 1, :], (8, F))) * inv
            for u in range(t, 16):
                col = jnp.broadcast_to(rows[u][:, j : j + 1], (8, F))
                if u == t:
                    if r == 7:
                        continue
                    below = sub > r
                    rows[u] = jnp.where(at & below, 0.0, rows[u]) - jnp.where(below, col, 0.0) * scaled
                else:
                    rows[u] = jnp.where(at, 0.0, rows[u]) - col * scaled
    out = []
    for rows in tiles:
        full = []
        for t in range(16):
            diag = lane == sub + 8 * t
            d = jnp.sum(jnp.where(diag, rows[t], 0.0), axis=1, keepdims=True)
            keep = jnp.where(lane < sub + 8 * t, rows[t], jnp.where(diag, 1.0, 0.0))
            full.append(keep * jnp.broadcast_to(1.0 / jnp.sqrt(d), (8, F)))
        out.append(jnp.concatenate(full, axis=0))
    return out


def solve_body(sum_ref, tail_ref, image_ref, next_ref, ritz_ref, mat_ref, inv_ref, *, total_rows):
    scale = 1.0 / total_rows
    sub = lax.broadcasted_iota(jnp.int32, (F, F), 0)
    lane = lax.broadcasted_iota(jnp.int32, (F, F), 1)

    def unpack(m, half):
        b21 = sum_ref[m * 32 : m * 32 + 16].reshape(F, F) * half
        both = sum_ref[m * 32 + 16 : m * 32 + 32].reshape(F, F) * half
        flip = both.T
        b11 = jnp.where(sub >= lane, both, flip)
        diag = jnp.broadcast_to(tail_ref[m : m + 1, :] * half, (F, F))
        b22 = jnp.where(sub < lane, both, jnp.where(sub == lane, diag, flip))
        return b11, b21, b22

    s11, s21, s22 = unpack(0, scale)
    w11, w21, w22 = unpack(2, scale)
    mat_ref[0] = s11
    mat_ref[1] = w11
    for n, (b21, b22) in enumerate(((s21, s22), (w21, w22))):
        mat_ref[2 + 2 * n] = b21
        mat_ref[3 + 2 * n] = b22

    def half_step(step, carry):
        s, w = eliminate([mat_ref[0], mat_ref[1]])
        for n, top in enumerate((s, w)):
            inv_ref[2 * step + n] = top

        @pl.when(step == 0)
        def _():
            for n, top in enumerate((s, w)):
                left = dot32(mat_ref[2 + 2 * n], top, NT)
                mat_ref[n] = mat_ref[3 + 2 * n] - dot32(left, left, NT)
                mat_ref[2 + 2 * n] = left

        return carry

    lax.fori_loop(0, 2, half_step, 0)

    def whole(n):
        top, low = inv_ref[n], inv_ref[2 + n]
        corner = -dot32(low, dot32(mat_ref[2 + 2 * n], top, NN), NN)
        return jnp.concatenate(
            [jnp.concatenate([top, jnp.zeros((F, F), jnp.float32)], axis=1), jnp.concatenate([corner, low], axis=1)], axis=0
        )

    q11, q21, q22 = unpack(1, 0.5 * scale)
    cross_sum = jnp.concatenate([jnp.concatenate([q11, q21.T], axis=1), jnp.concatenate([q21, q22], axis=1)], axis=0)
    s_inv = whole(0)
    ritz_ref[...] = dot32(dot32(s_inv, cross_sum, NN), s_inv, NT)
    w_inv = whole(1)
    for j in range(6):
        next_ref[:, j * K : (j + 1) * K] = dot32(image_ref[j * F : (j + 1) * F, :], w_inv, NT)


def solve(sums, tail, image, total_rows):
    return pl.pallas_call(
        functools.partial(solve_body, total_rows=total_rows),
        out_shape=(jax.ShapeDtypeStruct((F, 6 * K), jnp.float32), jax.ShapeDtypeStruct((K, K), jnp.float32)),
        in_specs=[VM] * 3,
        out_specs=(VM, VM),
        scratch_shapes=[pltpu.VMEM((6, F, F), jnp.float32), pltpu.VMEM((4, F, F), jnp.float32)],
        compiler_params=pltpu.CompilerParams(vmem_limit_bytes=BIG),
        name="solve",
    )(sums, tail, image)


def padded(cells, sides):
    for axis, dim in sides:
        count = lax.axis_size(axis)
        ring = [(i, (i + 1) % count) for i in range(count)]
        last = cells.shape[dim] - 1
        head = lax.slice_in_dim(cells, 0, 1, axis=dim)
        tail = lax.slice_in_dim(cells, last, last + 1, axis=dim)
        cells = jnp.concatenate(
            [lax.ppermute(tail, axis, ring), cells, lax.ppermute(head, axis, [(j, i) for i, j in ring])], axis=dim
        )
    return cells


def per_device(coordinates, neighbours, pair_index, pair_live, basis):
    own = coordinates[0, 0, 0].reshape(48, F)
    rows = extended(basis[0, 0, 0], own)
    near = padded(rows[None, None, None, :32], (("gz", 2), ("gy", 1), ("gx", 0)))
    hist = count_pairs(pair_index[0, 0, 0], pair_live[0, 0, 0].reshape(1, -1))
    table = jnp.concatenate([near.reshape(27 * 32, rows.shape[1]), rows], axis=0)
    image, gram = apply_pairs(hist, table, neighbours[0, 0, 0], own)
    sums, tail = total_grams(gram)
    next_rows, ritz = solve(sums, tail, image, 6.0 * F * 256)
    return next_rows.reshape(1, 1, 1, F, 6 * K), ritz


def solution(mesh):
    cells = [P("gx", "gy", "gz", *([None] * n)) for n in (3, 2, 2, 1, 2)]
    return jax.shard_map(per_device, mesh=mesh, in_specs=tuple(cells), out_specs=(cells[4], P()), check_vma=False)
```

time: 1220 us -> 159 us (0.13); the launches traced: 1200 us -> 159 us
  other arithmetic: 469 us -> 4.35 us
  local copies, waits for them, and re-layouts: 394 us -> 3.94 us
  waiting for transfers between devices: 268 us -> 12.9 us
  Pallas kernels: 0 us -> 127 us
  starting transfers between devices: 34.7 us -> 10.4 us
  between operations: 17.4 us -> 0.7 us
    gather x25 -> x0, local copies, waits for them, and re-layouts: 342 us -> none  [the longest x1 84.9 us: assemble(): jnp.take(neighbours.reshape(-1), slot_of * frames + own_frame, axis=0)]
    psum x1 -> x0, waiting for transfers between devices: 220 us -> none  [sum_in_two_steps(): own = lax.psum(own, far)]
    scatter-add x1 -> x0, other arithmetic: 164 us -> none  [assemble(): jnp.zeros((slots * frames, 36), jnp.float32).at[row_keys].add(values)]
    add x97 -> x0, other arithmetic: 162 us -> none  [the longest x96 161 us: add_slot(): total = total + column * pieces[inner_dof].astype(jnp.float32)]
    pallas_call x0 -> x4, Pallas kernels: none -> 127 us  [the longest x1 44.3 us: total_grams(): pl.pallas_call(total_body, out_shape=(jax.ShapeDtypeStruct((96, 8, F), jn...]
    another operation x21 -> x0, other arithmetic: 109 us -> none  [the longest x7 34.7 us: rayleigh_ritz(): factor = jnp.linalg.cholesky(basis_gram / total_rows)]
    reduce_scatter x3 -> x0, waiting for transfers between devices: 38.7 us -> none  [sum_in_two_steps(): own = lax.psum_scatter(padded, near, scatter_dimension=0, tiled=True)]
    ppermute x12 -> x6, starting transfers between devices: 34.5 us -> 10.4 us  [the longest x3 9.1 us: padded(): lax.ppermute(head, axis, [(j, i) for i, j in ring])]
  transfers between devices with their start and end apart: 16 -> 6, of which waited for: 6 -> 5; matrix products, arithmetic and copies ran while one was open for 62% -> 0% of each run, Pallas kernels for 0% -> 10%
where the time goes in v1:
time: 159 us
  Pallas kernels  127 us (80%)
  waiting for transfers between devices  12.9 us (8%)
  starting transfers between devices  10.4 us (7%)
  other arithmetic  4.35 us (3%)
  local copies, waits for them, and re-layouts  3.94 us (2%)
    pallas_call x1, Pallas kernels, total_grams(): pl.pallas_call(total_body, out_shape=(jax.ShapeDtypeStruct((96, 8, F), jn...  44.3 us
    pallas_call x1, Pallas kernels, solve(): pl.pallas_call(functools.partial(solve_body, total_rows=total_rows), out_...  40.4 us
    pallas_call x1, Pallas kernels, apply_pairs(): pl.pallas_call(apply_body, out_shape=(jax.ShapeDtypeStruct((6 * F, K), jn...  25.9 us
    pallas_call x1, Pallas kernels, count_pairs(): pl.pallas_call(count_body, out_shape=jax.ShapeDtypeStruct((4096, 128), jn...  16.1 us
    ppermute x3, starting transfers between devices, padded(): lax.ppermute(head, axis, [(j, i) for i, j in ring])  9.1 us
    ppermute x3, waiting for transfers between devices, padded(): lax.ppermute(head, axis, [(j, i) for i, j in ring])  6.58 us
    ppermute x3, waiting for transfers between devices, padded(): lax.ppermute(tail, axis, ring)  6.34 us
  transfers between devices with their start and end apart: 6, of which 5 were waited for; matrix products, arithmetic and copies ran while one was open for 0% of the time, Pallas kernels for 10%

profile of v1, /device:TPU:1, one launch (start us, length us, event | category | flops | bytes accessed | tf_op | source)
XLA Modules:
  0.0 159.0 jit_solution(11378068976657542638)
XLA Ops:
  0.6 0.7 fusion
  1.4 0.1 copy.9
  1.5 0.1 copy.8
  1.6 0.1 copy.7
  1.8 1.1 concatenate.15
  2.9 3.3 %collective-permute-start.1 = (bf16[1,1,1,32,1792]{4,3,2,1,0:T(8,128)(2,1)S(1)}, bf16[1,1,1,32,1792]{4,3,2,1,0:T(8,128)(2,1)S(1)}, u32[]{:S(2)}, u32[]{:S(2)}) collective-permute-start(bf16[1,1,1,32,1792]{4,3,2,1,0:T(8,128)(2,1)S(1)} %slice_bitcast_fusion), channel_id=1, source_target_pairs={{1,0},{2,1},{3,2},{4,3},{5,4},{6,5},{7,6},{0,7},{9,8},{10,9},{11,1... | collective-permute-start | bytes 344072 | tf_op jit(solution)/shard_map/ppermute | solution.py:467
  6.2 1.3 collective-permute-start
  7.4 2.4 %collective-permute-done.1 = bf16[1,1,1,32,1792]{4,3,2,1,0:T(8,128)(2,1)S(1)} collective-permute-done((bf16[1,1,1,32,1792]{4,3,2,1,0:T(8,128)(2,1)S(1)}, bf16[1,1,1,32,1792]{4,3,2,1,0:T(8,128)(2,1)S(1)}, u32[]{:S(2)}, u32[]{:S(2)}) %collective-permute-start.1) | collective-permute-done | bytes 114720 | tf_op jit(solution)/shard_map/ppermute | solution.py:467
  9.8 1.2 collective-permute-done
  11.1 2.6 %collective-permute-start.3 = (bf16[1,1,3,32,1792]{4,3,2,1,0:T(8,128)(2,1)S(1)}, bf16[1,1,3,32,1792]{4,3,2,1,0:T(8,128)(2,1)S(1)}, u32[]{:S(2)}, u32[]{:S(2)}) collective-permute-start(bf16[1,1,3,32,1792]{4,3,2,1,0:T(8,128)(2,1)S(1)} %pad_maximum_fusion.3), channel_id=1, source_target_pairs={{8,0},{16,8},{24,16},{0,24},{9,1},{17,9},{25,17},{1,25},{10,2},{18... | collective-permute-start | bytes 1032200 | tf_op jit(solution)/shard_map/ppermute | solution.py:467
  13.6 0.0 collective-permute-start.2
  13.6 4.2 %collective-permute-done.3 = bf16[1,1,3,32,1792]{4,3,2,1,0:T(8,128)(2,1)S(1)} collective-permute-done((bf16[1,1,3,32,1792]{4,3,2,1,0:T(8,128)(2,1)S(1)}, bf16[1,1,3,32,1792]{4,3,2,1,0:T(8,128)(2,1)S(1)}, u32[]{:S(2)}, u32[]{:S(2)}) %collective-permute-start.3) | collective-permute-done | bytes 344096 | tf_op jit(solution)/shard_map/ppermute | solution.py:467
  17.8 3.1 %collective-permute-done.2 = bf16[1,1,3,32,1792]{4,3,2,1,0:T(8,128)(2,1)S(1)} collective-permute-done((bf16[1,1,3,32,1792]{4,3,2,1,0:T(8,128)(2,1)S(1)}, bf16[1,1,3,32,1792]{4,3,2,1,0:T(8,128)(2,1)S(1)}, u32[]{:S(2)}, u32[]{:S(2)}) %collective-permute-start.2) | collective-permute-done | bytes 344096 | tf_op jit(solution)/shard_map/ppermute | solution.py:467
  20.9 0.1 pad_maximum_fusion.2
  21.1 3.3 %collective-permute-start.5 = (bf16[1,3,3,32,1792]{4,3,2,1,0:T(8,128)(2,1)S(1)}, bf16[1,3,3,32,1792]{4,3,2,1,0:T(8,128)(2,1)S(1)}, u32[]{:S(2)}, u32[]{:S(2)}) collective-permute-start(bf16[1,3,3,32,1792]{4,3,2,1,0:T(8,128)(2,1)S(1)} %pad_maximum_fusion.2), channel_id=1, source_target_pairs={{32,0},{64,32},{96,64},{128,96},{160,128},{192,160},{224,192},{0,2... | collective-permute-start | bytes 3096584 | tf_op jit(solution)/shard_map/ppermute | solution.py:467
  24.3 0.0 collective-permute-start.4
  24.3 16.1 %count_pairs.1.hist_ref = f32[4096,128]{1,0:T(8,128)} custom-call(s32[4,15360]{1,0:T(4,128)} %bitcast.21, s32[1,15360]{1,0:T(1,128)} %bitcast.22), custom_call_target="tpu_custom_call" | custom-call | flops 8000000000 | bytes 3000000 | tf_op jit(solution)/shard_map/count_pairs/pallas_call | solution.py:70
  40.4 0.0 collective-permute-done.5
  40.4 2.0 %collective-permute-done.4 = bf16[1,3,3,32,1792]{4,3,2,1,0:T(8,128)(2,1)} collective-permute-done((bf16[1,3,3,32,1792]{4,3,2,1,0:T(8,128)(2,1)S(1)}, bf16[1,3,3,32,1792]{4,3,2,1,0:T(8,128)(2,1)}, u32[]{:S(2)}, u32[]{:S(2)}) %collective-permute-start.4) | collective-permute-done | bytes 1032224 | tf_op jit(solution)/shard_map/ppermute | solution.py:467
  42.5 1.4 pad_maximum_fusion.1
  43.9 2.0 %pad_maximum_fusion.table_ref = bf16[992,1792]{1,0:T(8,128)(2,1)} fusion(bf16[128,1792]{1,0:T(8,128)(2,1)S(1)} %concatenate.15, bf16[864,1792]{1,0:T(8,128)(2,1)S(1)} %bitcast.17), kind=kLoop, calls=%fused_computation | loop fusion | flops 7110656 | bytes 7110656 | tf_op jit(solution)/shard_map/concatenate | solution.py:477
  45.9 25.9 %apply_pairs.1 = (f32[768,256]{1,0:T(8,128)}, f32[768,256]{1,0:T(8,128)}) custom-call(f32[4096,128]{1,0:T(8,128)} %count_pairs.1.hist_ref, bf16[992,1792]{1,0:T(8,128)(2,1)} %pad_maximum_fusion.table_ref, s32[16,128]{1,0:T(8,128)} %bitcast.23, f32[48,128]{1,0:T(8,128)} %bitcast.19), custom_call_target="tpu_custom_call" | custom-call | flops 8000000000 | bytes 8000000 | tf_op jit(solution)/shard_map/apply_pairs/pallas_call | solution.py:209
  71.8 0.0 copy-start
  71.8 1.1 copy-done
  72.9 44.3 %total_grams.1 = (f32[96,8,128]{2,1,0:T(8,128)S(1)}, f32[8,128]{1,0:T(8,128)S(1)}) custom-call(f32[768,256]{1,0:T(8,128)S(1)} %copy-done), custom_call_target="tpu_custom_call" | custom-call | flops 1000000 | bytes 2000000 | tf_op jit(solution)/shard_map/total_grams/pallas_call | solution.py:338
  117.3 0.0 copy-start.1
  117.3 0.7 copy-done.1
  118.0 0.0 copy-start.2
  118.0 0.6 copy-done.2
  118.6 40.4 %solve.1 = (f32[128,1536]{1,0:T(8,128)}, f32[256,256]{1,0:T(8,128)}) custom-call(f32[96,8,128]{2,1,0:T(8,128)} %copy-done.1, f32[8,128]{1,0:T(8,128)} %copy-done.2, f32[768,256]{1,0:T(8,128)} %get-tuple-element.11.image_ref), custom_call_target="tpu_custom_call" | custom-call | tf_op jit(solution)/shard_map/solve/pallas_call | solution.py:448
  (3 shorter events, 0.1 us)
Async XLA Ops:
  2.9 6.9 %collective-permute-start.1 = (bf16[1,1,1,32,1792]{4,3,2,1,0:T(8,128)(2,1)S(1)}, bf16[1,1,1,32,1792]{4,3,2,1,0:T(8,128)(2,1)S(1)}, u32[]{:S(2)}, u32[]{:S(2)}) collective-permute-start(bf16[1,1,1,32,1792]{4,3,2,1,0:T(8,128)(2,1)S(1)} %slice_bitcast_fusion), channel_id=1, source_target_pairs={{1,0},{2,1},{3,2},{4,3},{5,4},{6,5},{7,6},{0,7},{9,8},{10,9},{11,1... | collective-permute-start | bytes 344072 | tf_op jit(solution)/shard_map/ppermute | solution.py:467
  6.2 4.8 %collective-permute-start = (bf16[1,1,1,32,1792]{4,3,2,1,0:T(8,128)(2,1)S(1)}, bf16[1,1,1,32,1792]{4,3,2,1,0:T(8,128)(2,1)S(1)}, u32[]{:S(2)}, u32[]{:S(2)}) collective-permute-start(bf16[1,1,1,32,1792]{4,3,2,1,0:T(8,128)(2,1)S(1)} %slice_bitcast_fusion), channel_id=1, source_target_pairs={{0,1},{1,2},{2,3},{3,4},{4,5},{5,6},{6,7},{7,0},{8,9},{9,10},{10,1... | collective-permute-start | bytes 344072 | tf_op jit(solution)/shard_map/ppermute | solution.py:467
  11.1 6.8 %collective-permute-start.3 = (bf16[1,1,3,32,1792]{4,3,2,1,0:T(8,128)(2,1)S(1)}, bf16[1,1,3,32,1792]{4,3,2,1,0:T(8,128)(2,1)S(1)}, u32[]{:S(2)}, u32[]{:S(2)}) collective-permute-start(bf16[1,1,3,32,1792]{4,3,2,1,0:T(8,128)(2,1)S(1)} %pad_maximum_fusion.3), channel_id=1, source_target_pairs={{8,0},{16,8},{24,16},{0,24},{9,1},{17,9},{25,17},{1,25},{10,2},{18... | collective-permute-start | bytes 1032200 | tf_op jit(solution)/shard_map/ppermute | solution.py:467
  13.6 7.3 %collective-permute-start.2 = (bf16[1,1,3,32,1792]{4,3,2,1,0:T(8,128)(2,1)S(1)}, bf16[1,1,3,32,1792]{4,3,2,1,0:T(8,128)(2,1)S(1)}, u32[]{:S(2)}, u32[]{:S(2)}) collective-permute-start(bf16[1,1,3,32,1792]{4,3,2,1,0:T(8,128)(2,1)S(1)} %pad_maximum_fusion.3), channel_id=1, source_target_pairs={{0,8},{8,16},{16,24},{24,0},{1,9},{9,17},{17,25},{25,1},{2,10},{10... | collective-permute-start | bytes 1032200 | tf_op jit(solution)/shard_map/ppermute | solution.py:467
  21.1 19.4 %collective-permute-start.5 = (bf16[1,3,3,32,1792]{4,3,2,1,0:T(8,128)(2,1)S(1)}, bf16[1,3,3,32,1792]{4,3,2,1,0:T(8,128)(2,1)S(1)}, u32[]{:S(2)}, u32[]{:S(2)}) collective-permute-start(bf16[1,3,3,32,1792]{4,3,2,1,0:T(8,128)(2,1)S(1)} %pad_maximum_fusion.2), channel_id=1, source_target_pairs={{32,0},{64,32},{96,64},{128,96},{160,128},{192,160},{224,192},{0,2... | collective-permute-start | bytes 3096584 | tf_op jit(solution)/shard_map/ppermute | solution.py:467
  24.3 18.1 %collective-permute-start.4 = (bf16[1,3,3,32,1792]{4,3,2,1,0:T(8,128)(2,1)S(1)}, bf16[1,3,3,32,1792]{4,3,2,1,0:T(8,128)(2,1)}, u32[]{:S(2)}, u32[]{:S(2)}) collective-permute-start(bf16[1,3,3,32,1792]{4,3,2,1,0:T(8,128)(2,1)S(1)} %pad_maximum_fusion.2), channel_id=1, source_target_pairs={{0,32},{32,64},{64,96},{96,128},{128,160},{160,192},{192,224},{224... | collective-permute-start | bytes 3096584 | tf_op jit(solution)/shard_map/ppermute | solution.py:467
  71.8 1.1 copy-start
  117.3 0.7 copy-start.1
  118.0 0.6 copy-start.2

commit v2 on v1

--- a/solution.py
+++ b/solution.py
@@ -16,33 +16,34 @@
 STEP = 768
 
 
-def count_body(pairs_ref, live_ref, hist_ref, acc_ref):
+def counter(pairs_ref, live_ref, hist_ref, acc_ref):
     rows = lax.broadcasted_iota(jnp.int32, (256, STEP), 0)
     zero = jnp.zeros((256, STEP), jnp.float32)
 
-    def chunk(c, first):
-        def step(t, carry):
-            at = pl.ds(pl.multiple_of(c * CHUNK + t * STEP, 128), STEP)
-            f = pairs_ref[0:1, at]
-            s = pairs_ref[1:2, at]
-            a = pairs_ref[2:3, at]
-            b = pairs_ref[3:4, at]
-            live = live_ref[0:1, at]
-            value = (live * jnp.where(a >= 8, int(PB), 1)).astype(jnp.float32)
-            col = ((a >> 2) & 1) * 128 + f
-            right = jnp.where(rows == col, jnp.broadcast_to(value, (256, STEP)), zero).astype(jnp.bfloat16)
-            hot = rows == (b * 16 + s)
-            low = a & 3
-            for part in range(4):
-                mark = jnp.broadcast_to((low == part).astype(jnp.float32), (256, STEP))
-                left = jnp.where(hot, mark, zero).astype(jnp.bfloat16)
-                got = lax.dot_general(left, right, (((1,), (1,)), ((), ())), preferred_element_type=jnp.float32)
-                here = pl.ds(part * 256, 256)
-                acc_ref[here, :] = acc_ref[here, :] + got
-            return carry
-
+    def step(at, carry):
+        at = pl.ds(pl.multiple_of(at * STEP, 128), STEP)
+        f = pairs_ref[0:1, at]
+        s = pairs_ref[1:2, at]
+        a = pairs_ref[2:3, at]
+        b = pairs_ref[3:4, at]
+        live = live_ref[0:1, at]
+        value = (live * jnp.where(a >= 8, int(PB), 1)).astype(jnp.float32)
+        col = ((a >> 2) & 1) * 128 + f
+        right = jnp.where(rows == col, jnp.broadcast_to(value, (256, STEP)), zero).astype(jnp.bfloat16)
+        hot = rows == (b * 16 + s)
+        low = a & 3
+        for part in range(4):
+            mark = jnp.broadcast_to((low == part).astype(jnp.float32), (256, STEP))
+            left = jnp.where(hot, mark, zero).astype(jnp.bfloat16)
+            got = lax.dot_general(left, right, (((1,), (1,)), ((), ())), preferred_element_type=jnp.float32)
+            here = pl.ds(part * 256, 256)
+            acc_ref[here, :] = acc_ref[here, :] + got
+        return carry
+
+    def chunk(c):
         acc_ref[...] = jnp.zeros_like(acc_ref)
-        lax.fori_loop(0, CHUNK // STEP, step, 0)
+        steps = CHUNK // STEP
+        lax.fori_loop(c * steps, (c + 1) * steps, step, 0)
         for part in range(4):
             got = acc_ref[part * 256 : (part + 1) * 256, :]
             high = jnp.floor(got * (1.0 / PB))
@@ -52,31 +53,12 @@
                 for top, val in ((0, lower), (1, high)):
                     a = top * 8 + mid * 4 + part
                     here = slice(a * 256, (a + 1) * 256)
-                    if first:
+                    if c == 0:
                         hist_ref[here, :] = val[:, lanes]
                     else:
                         hist_ref[here, :] = hist_ref[here, :] + val[:, lanes]
 
-    chunk(0, True)
-
-    def more(c, carry):
-        chunk(c, False)
-        return carry
-
-    lax.fori_loop(1, pairs_ref.shape[1] // CHUNK, more, 0)
-
-
-def count_pairs(pairs, live):
-    return pl.pallas_call(
-        count_body,
-        out_shape=jax.ShapeDtypeStruct((4096, 128), jnp.float32),
-        in_specs=[VM, VM],
-        out_specs=VM,
-        scratch_shapes=[pltpu.VMEM((1024, 256), jnp.float32)],
-        compiler_params=pltpu.CompilerParams(vmem_limit_bytes=BIG),
-        cost_estimate=pl.CostEstimate(flops=8 * 10**9, bytes_accessed=3 * 10**6, transcendentals=0),
-        name="count_pairs",
-    )(pairs, live)
+    return chunk
 
 
 def cross(p, q):
@@ -226,22 +208,6 @@
         name="apply_pairs",
     )(hist, table, lists, coords)
 
-
-def three_parts(rows):
-    def cut(x):
-        return lax.reduce_precision(x, 8, 7)
-
-    high = cut(rows)
-    mid = cut(rows - high)
-    low = rows - high - mid
-    return jnp.concatenate([high.astype(jnp.bfloat16), mid.astype(jnp.bfloat16), low.astype(jnp.bfloat16)], axis=1)
-
-
-def extended(basis, coords):
-    frames = basis.shape[0]
-    flat = coords.reshape(48, frames).T
-    parts = three_parts(flat)
-    return jnp.concatenate([basis, parts, jnp.zeros((frames, 256 - 144), jnp.bfloat16)], axis=1)
 
 MESH = pl.DeviceIdType.MESH
 
@@ -350,6 +316,96 @@
     )(gram)
 
 
+def near_body(pairs_ref, live_ref, basis_ref, coords_ref, hist_ref, table_ref, acc_ref, send, recv):
+    gx, gy, gz = lax.axis_index("gx"), lax.axis_index("gy"), lax.axis_index("gz")
+    core = lax.rem(gz, 2)
+    far = 2 * core
+    partner = {"gz": gz + 1 - 2 * core}
+    beyond = {"gz": lax.rem(gz + 7 + 2 * core, 8)}
+    up_x, down_x = {"gy": lax.rem(gy + 1, 4)}, {"gy": lax.rem(gy + 3, 4)}
+    up_y, down_y = {"gx": lax.rem(gx + 1, 8)}, {"gx": lax.rem(gx + 7, 8)}
+    barrier = pltpu.get_barrier_semaphore()
+    for peer in (partner, beyond, up_x, down_x, up_y, down_y):
+        pl.semaphore_signal(barrier, inc=1, device_id=peer, device_id_type=MESH)
+
+    own = 27 * 32
+    flat = coords_ref[...]
+    high = flat.astype(jnp.bfloat16).astype(jnp.float32)
+    mid = (flat - high).astype(jnp.bfloat16).astype(jnp.float32)
+    parts = jnp.concatenate([high, mid, flat - high - mid, jnp.zeros((112, F), jnp.float32)], axis=0)
+    table_ref[own : own + F, 0 : 6 * K] = basis_ref[...]
+    table_ref[own : own + F, 6 * K : 7 * K] = jnp.transpose(parts).astype(jnp.bfloat16)
+    table_ref[13 * 32 : 14 * 32, :] = table_ref[own : own + 32, :]
+    pl.semaphore_wait(barrier, 6)
+
+    count = [0]
+
+    def slab(a, b, e):
+        return table_ref.at[pl.ds(pl.multiple_of((9 * a + 3 * b + e) * 32, 32), 32)]
+
+    def copy(src, dst, peer):
+        n = count[0]
+        count[0] += 1
+        c = pltpu.make_async_remote_copy(src_ref=src, dst_ref=dst, send_sem=send.at[n], recv_sem=recv.at[n], device_id=peer, device_id_type=MESH)
+        c.start()
+        return c
+
+    def first_hops(e):
+        return [
+            copy(slab(1, 1, e), slab(1, 0, e), up_x),
+            copy(slab(1, 1, e), slab(1, 2, e), down_x),
+            copy(slab(1, 1, e), slab(0, 1, e), up_y),
+            copy(slab(1, 1, e), slab(2, 1, e), down_y),
+        ]
+
+    def second_hops(e):
+        return [
+            copy(slab(1, 0, e), slab(0, 0, e), up_y),
+            copy(slab(1, 2, e), slab(2, 2, e), down_y),
+            copy(slab(0, 1, e), slab(0, 2, e), down_x),
+            copy(slab(2, 1, e), slab(2, 0, e), up_x),
+        ]
+
+    def forward(places):
+        return [copy(slab(a, b, 1), slab(a, b, far), partner) for a, b in places]
+
+    edges, corners = ((1, 0), (1, 2), (0, 1), (2, 1)), ((0, 0), (2, 2), (0, 2), (2, 0))
+    z_far = copy(slab(1, 1, 1), slab(1, 1, 2 - far), beyond)
+    z_near = copy(slab(1, 1, 1), slab(1, 1, far), partner)
+    own_first = first_hops(1)
+    chunk = counter(pairs_ref, live_ref, hist_ref, acc_ref)
+    chunk(0)
+    for c in [z_far] + own_first:
+        c.wait_recv()
+    far_first = first_hops(far)
+    own_second = second_hops(1)
+    sent = forward(edges)
+    chunk(1)
+    for c in own_second + far_first:
+        c.wait_recv()
+    far_second = second_hops(far)
+    sent = sent + forward(corners)
+    chunk(2)
+    chunk(3)
+    for c in [z_near] + far_second + sent:
+        c.wait_recv()
+    for c in [z_far, z_near] + own_first + far_first + own_second + far_second + sent:
+        c.wait_send()
+
+
+def near_and_counts(pairs, live, basis, coords):
+    return pl.pallas_call(
+        near_body,
+        out_shape=(jax.ShapeDtypeStruct((4096, F), jnp.float32), jax.ShapeDtypeStruct((27 * 32 + F, 7 * K), jnp.bfloat16)),
+        in_specs=[VM] * 4,
+        out_specs=(VM, VM),
+        scratch_shapes=[pltpu.VMEM((1024, 256), jnp.float32), pltpu.SemaphoreType.DMA((26,)), pltpu.SemaphoreType.DMA((26,))],
+        compiler_params=pltpu.CompilerParams(collective_id=2, has_side_effects=True, vmem_limit_bytes=BIG),
+        cost_estimate=pl.CostEstimate(flops=8 * 10**9, bytes_accessed=3 * 10**6, transcendentals=0),
+        name="near_and_counts",
+    )(pairs, live, basis, coords)
+
+
 def dot32(p, q, dims):
     return lax.dot_general(p, q, (dims, ((), ())), precision=lax.Precision.HIGHEST, preferred_element_type=jnp.float32)
 
@@ -456,25 +512,9 @@
     )(sums, tail, image)
 
 
-def padded(cells, sides):
-    for axis, dim in sides:
-        count = lax.axis_size(axis)
-        ring = [(i, (i + 1) % count) for i in range(count)]
-        last = cells.shape[dim] - 1
-        head = lax.slice_in_dim(cells, 0, 1, axis=dim)
-        tail = lax.slice_in_dim(cells, last, last + 1, axis=dim)
-        cells = jnp.concatenate(
-            [lax.ppermute(tail, axis, ring), cells, lax.ppermute(head, axis, [(j, i) for i, j in ring])], axis=dim
-        )
-    return cells
-
-
 def per_device(coordinates, neighbours, pair_index, pair_live, basis):
     own = coordinates[0, 0, 0].reshape(48, F)
-    rows = extended(basis[0, 0, 0], own)
-    near = padded(rows[None, None, None, :32], (("gz", 2), ("gy", 1), ("gx", 0)))
-    hist = count_pairs(pair_index[0, 0, 0], pair_live[0, 0, 0].reshape(1, -1))
-    table = jnp.concatenate([near.reshape(27 * 32, rows.shape[1]), rows], axis=0)
+    hist, table = near_and_counts(pair_index[0, 0, 0], pair_live[0, 0, 0].reshape(1, -1), basis[0, 0, 0], own)
     image, gram = apply_pairs(hist, table, neighbours[0, 0, 0], own)
     sums, tail = total_grams(gram)
     next_rows, ritz = solve(sums, tail, image, 6.0 * F * 256)

time: 159 us -> 133 us (0.84)
  waiting for transfers between devices: 12.9 us -> 0 us
  starting transfers between devices: 10.4 us -> 0 us
  other arithmetic: 4.35 us -> 0 us
  Pallas kernels: 127 us -> 130 us
    pallas_call x1, Pallas kernels: 16.1 us -> 30.9 us  [near_and_counts(): pl.pallas_call(near_body, out_shape=(jax.ShapeDtypeStruct((4096, F), jnp....]
    ppermute x6 -> x0, waiting for transfers between devices: 12.9 us -> none  [the longest x3 6.58 us: padded(): lax.ppermute(head, axis, [(j, i) for i, j in ring])]
    pallas_call x1, Pallas kernels: 44.3 us -> 32.6 us  [total_grams(): pl.pallas_call(total_body, out_shape=(jax.ShapeDtypeStruct((96, 8, F), jn...]
    ppermute x6 -> x0, starting transfers between devices: 10.4 us -> none  [the longest x3 9.1 us: padded(): lax.ppermute(head, axis, [(j, i) for i, j in ring])]
    concatenate x4 -> x0, other arithmetic: 3.6 us -> none  [the longest x1 1.99 us: per_device(): jnp.concatenate([near.reshape(27 * 32, rows.shape[1]), rows], axis=0)]
  transfers between devices with their start and end apart: 6 -> 0, of which waited for: 5 -> 0; matrix products, arithmetic and copies ran while one was open for 0% -> 0% of each run, Pallas kernels for 10% -> 0%
where the time goes in v2:
time: 133 us
  Pallas kernels  130 us (98%)
  local copies, waits for them, and re-layouts  2.47 us (2%)
    pallas_call x1, Pallas kernels, solve(): pl.pallas_call(functools.partial(solve_body, total_rows=total_rows), out_...  40.4 us
    pallas_call x1, Pallas kernels, total_grams(): pl.pallas_call(total_body, out_shape=(jax.ShapeDtypeStruct((96, 8, F), jn...  32.6 us
    pallas_call x1, Pallas kernels, near_and_counts(): pl.pallas_call(near_body, out_shape=(jax.ShapeDtypeStruct((4096, F), jnp....  30.9 us
    pallas_call x1, Pallas kernels, apply_pairs(): pl.pallas_call(apply_body, out_shape=(jax.ShapeDtypeStruct((6 * F, K), jn...  25.9 us

profile of v2, /device:TPU:1, one launch (start us, length us, event | category | flops | bytes accessed | tf_op | source)
XLA Modules:
  0.0 132.9 jit_solution(8645121780312098142)
XLA Ops:
  0.6 30.9 %near_and_counts.1 = (f32[4096,128]{1,0:T(8,128)}, bf16[992,1792]{1,0:T(8,128)(2,1)}) custom-call(s32[4,15360]{1,0:T(4,128)} %bitcast.8, s32[1,15360]{1,0:T(1,128)} %bitcast.9, bf16[128,1536]{1,0:T(8,128)(2,1)} %bitcast.7, f32[48,128]{1,0:T(8,128)} %bitcast.10), custom_call_target="tpu_custom_call" | custom-call | flops 8000000000 | bytes 3000000 | tf_op jit(solution)/shard_map/near_and_counts/pallas_call | solution.py:397
  31.5 25.9 %apply_pairs.1 = (f32[768,256]{1,0:T(8,128)}, f32[768,256]{1,0:T(8,128)}) custom-call(f32[4096,128]{1,0:T(8,128)} %get-tuple-element.10.hist_ref, bf16[992,1792]{1,0:T(8,128)(2,1)} %get-tuple-element.11.table_ref, s32[16,128]{1,0:T(8,128)} %bitcast.12, f32[48,128]{1,0:T(8,128)} %bitcast.11), custom_call_target="tpu_custom_call" | custom-call | flops 8000000000 | bytes 8000000 | tf_op jit(solution)/shard_map/apply_pairs/pallas_call | solution.py:191
  57.4 0.0 copy-start
  57.4 1.1 copy-done
  58.5 32.6 %total_grams.1 = (f32[96,8,128]{2,1,0:T(8,128)S(1)}, f32[8,128]{1,0:T(8,128)S(1)}) custom-call(f32[768,256]{1,0:T(8,128)S(1)} %copy-done), custom_call_target="tpu_custom_call" | custom-call | flops 1000000 | bytes 2000000 | tf_op jit(solution)/shard_map/total_grams/pallas_call | solution.py:304
  91.1 0.0 copy-start.1
  91.1 0.7 copy-done.1
  91.9 0.0 copy-start.2
  91.9 0.6 copy-done.2
  92.5 40.4 %solve.1 = (f32[128,1536]{1,0:T(8,128)}, f32[256,256]{1,0:T(8,128)}) custom-call(f32[96,8,128]{2,1,0:T(8,128)} %copy-done.1, f32[8,128]{1,0:T(8,128)} %copy-done.2, f32[768,256]{1,0:T(8,128)} %get-tuple-element.15.image_ref), custom_call_target="tpu_custom_call" | custom-call | tf_op jit(solution)/shard_map/solve/pallas_call | solution.py:504
Async XLA Ops:
  57.4 1.1 copy-start
  91.1 0.8 copy-start.1
  91.9 0.6 copy-start.2

commit v3 on v2

--- a/solution.py
+++ b/solution.py
@@ -7,7 +7,6 @@
 from jax.sharding import PartitionSpec as P
 
 VM = pl.BlockSpec(memory_space=pltpu.VMEM)
-BIG = 60 * 1024 * 1024
 F = 128
 K = 256
 NB = 16
@@ -203,7 +202,7 @@
             pltpu.VMEM((6 * F, K), jnp.bfloat16),
             pltpu.VMEM((6 * F, K), jnp.bfloat16),
         ],
-        compiler_params=pltpu.CompilerParams(vmem_limit_bytes=BIG),
+        compiler_params=pltpu.CompilerParams(vmem_limit_bytes=36 * 1024 * 1024),
         cost_estimate=pl.CostEstimate(flops=8 * 10**9, bytes_accessed=8 * 10**6, transcendentals=0),
         name="apply_pairs",
     )(hist, table, lists, coords)
@@ -222,19 +221,21 @@
     return {"gx": lax.rem(z, 2) * 4 + y, "gy": x, "gz": lax.div(z, 2) * 2 + core}
 
 
-def total_body(gram_ref, out_ref, tail_ref, data, half_in, half, y_in, part, x_in, z_in, t1, t2, t3, t4, send, recv):
+PLANE = [(dx, dy) for dx in (2, 1, 3, 0) for dy in (2, 1, 3, 0)][:15]
+
+
+def total_body(gram_ref, out_ref, tail_ref, data, half_in, half, plane_in, z_in, t1, t3, t4, send, recv):
     x, y, z, core = place()
-    across = [device(x, y, z, 1 - core)]
-    along_y = [device(x, lax.rem(y + d, 4), z, core) for d in range(1, 4)]
-    along_x = [device(lax.rem(x + d, 4), y, z, core) for d in range(1, 4)]
+    partner = device(x, y, z, 1 - core)
+    plane = [device(lax.rem(x + dx, 4), lax.rem(y + dy, 4), z, core) for dx, dy in PLANE]
     along_z = [device(x, y, lax.rem(z + d, 8), core) for d in range(1, 8)]
     barrier = pltpu.get_barrier_semaphore()
-    for peer in across + along_y + along_x + along_z:
+    for peer in [partner] + plane + along_z:
         pl.semaphore_signal(barrier, inc=1, device_id=peer, device_id_type=MESH)
 
     lower = lax.broadcasted_iota(jnp.int32, (F, F), 0) >= lax.broadcasted_iota(jnp.int32, (F, F), 1)
     eye = lax.broadcasted_iota(jnp.int32, (F, F), 0) == lax.broadcasted_iota(jnp.int32, (F, F), 1)
-    t1[0] = jnp.zeros((8, F), jnp.float32)
+    t1[0] = jnp.zeros((4, F), jnp.float32)
     for m in range(3):
         b11 = gram_ref[m * K : m * K + F, 0:F]
         b21 = gram_ref[m * K + F : m * K + K, 0:F]
@@ -246,60 +247,83 @@
         data[m * 32 : m * 32 + 16] = b21.reshape(16, 8, F)
         data[m * 32 + 16 : m * 32 + 32] = jnp.where(lower, b11, b22).reshape(16, 8, F)
         t1[0, m : m + 1, :] = jnp.sum(jnp.where(eye, b22, 0.0), axis=0, keepdims=True)
-    pl.semaphore_wait(barrier, 14)
+    pl.semaphore_wait(barrier, 23)
 
     count = [0]
+    started = []
 
     def copy(src, dst, peer):
         n = count[0]
         count[0] += 1
-        return pltpu.make_async_remote_copy(src_ref=src, dst_ref=dst, send_sem=send.at[n], recv_sem=recv.at[n], device_id=peer, device_id_type=MESH)
-
-    def run(copies):
-        for c in copies:
-            c.start()
-        for c in copies:
-            c.wait()
-
-    run([
-        copy(data.at[pl.ds((1 - core) * 48, 48)], half_in, across[0]),
-        copy(t1.at[0], t1.at[1], across[0]),
-    ])
-    half[...] = data[pl.ds(core * 48, 48)] + half_in[...]
-    t2[y] = t1[0] + t1[1]
-    run(
-        [copy(half.at[pl.ds(lax.rem(y + d, 4) * 12, 12)], y_in.at[d - 1], along_y[d - 1]) for d in range(1, 4)]
-        + [copy(t2.at[y], t2.at[y], along_y[d - 1]) for d in range(1, 4)]
-    )
-    part[...] = half[pl.ds(y * 12, 12)] + y_in[0] + y_in[1] + y_in[2]
-    t3[x] = t2[0] + t2[1] + t2[2] + t2[3]
-    run(
-        [copy(part.at[pl.ds(lax.rem(x + d, 4) * 3, 3)], x_in.at[d - 1], along_x[d - 1]) for d in range(1, 4)]
-        + [copy(t3.at[x], t3.at[x], along_x[d - 1]) for d in range(1, 4)]
-    )
-    z_in[z] = part[pl.ds(x * 3, 3)] + x_in[0] + x_in[1] + x_in[2]
-    t4[z] = t3[0] + t3[1] + t3[2] + t3[3]
-    run(
-        [copy(z_in.at[z], z_in.at[z], along_z[d - 1]) for d in range(1, 8)]
-        + [copy(t4.at[z], t4.at[z], along_z[d - 1]) for d in range(1, 8)]
-    )
-    total, tail = z_in[0], t4[0]
+        c = pltpu.make_async_remote_copy(src_ref=src, dst_ref=dst, send_sem=send.at[n], recv_sem=recv.at[n], device_id=peer, device_id_type=MESH)
+        c.start()
+        started.append(c)
+        return c
+
+    first = []
+    for dx in (2, 1, 3, 0):
+        at = lax.rem(x + dx, 4) * 12
+        first.append(copy(data.at[pl.ds((1 - core) * 48 + at, 12)], half_in.at[pl.ds(at, 12)], partner))
+    small = copy(t1.at[0], t1.at[1], partner)
+    arriving = []
+    for n, dx in enumerate((2, 1, 3, 0)):
+        at = lax.rem(x + dx, 4) * 12
+        first[n].wait_recv()
+        half[pl.ds(at, 12)] = data[pl.ds(core * 48 + at, 12)] + half_in[pl.ds(at, 12)]
+        for slot, (px, py) in enumerate(PLANE):
+            if px == dx:
+                piece = at + lax.rem(y + py, 4) * 3
+                arriving.append(copy(half.at[pl.ds(piece, 3)], plane_in.at[slot], plane[slot]))
+    small.wait_recv()
+    here = x * 4 + y
+    t3[here] = t1[0] + t1[1]
+    tails = [copy(t3.at[here], t3.at[here], plane[slot]) for slot in range(15)]
+    total = half[pl.ds(here * 3, 3)]
+    for slot in range(15):
+        arriving[slot].wait_recv()
+        total = total + plane_in[slot]
+    z_in[z] = total
+    arriving = [copy(z_in.at[z], z_in.at[z], along_z[d - 1]) for d in range(1, 8)]
+    for c in tails:
+        c.wait_recv()
+    tail = t3[0]
+    for n in range(1, 16):
+        tail = tail + t3[n]
+    t4[z] = tail
+    tails = [copy(t4.at[z], t4.at[z], along_z[d - 1]) for d in range(1, 8)]
+    for c in arriving:
+        c.wait_recv()
+    total = z_in[0]
     for n in range(1, 8):
         total = total + z_in[n]
+    mine = core * 48 + here * 3
+    out_ref[pl.ds(mine, 3)] = total
+    arriving = [copy(out_ref.at[pl.ds(mine, 3)], out_ref.at[pl.ds(mine, 3)], plane[slot]) for slot in range(15)]
+    onward = [copy(out_ref.at[pl.ds(mine, 3)], out_ref.at[pl.ds(mine, 3)], partner)]
+    for c in tails:
+        c.wait_recv()
+    tail = t4[0]
+    for n in range(1, 8):
         tail = tail + t4[n]
-    tail_ref[...] = tail
-    mine = core * 48 + y * 12 + x * 3
-    out_ref[pl.ds(mine, 3)] = total
-    run([copy(out_ref.at[pl.ds(mine, 3)], out_ref.at[pl.ds(mine, 3)], along_x[d - 1]) for d in range(1, 4)])
-    mine = core * 48 + y * 12
-    run([copy(out_ref.at[pl.ds(mine, 12)], out_ref.at[pl.ds(mine, 12)], along_y[d - 1]) for d in range(1, 4)])
-    mine = core * 48
-    run([copy(out_ref.at[pl.ds(mine, 48)], out_ref.at[pl.ds(mine, 48)], across[0])])
+    tail_ref[0:4, :] = tail
+    tail_ref[4:8, :] = tail
+    for slot in reversed(range(15)):
+        dx, dy = PLANE[slot]
+        theirs = core * 48 + (lax.rem(x + 4 - dx, 4) * 4 + lax.rem(y + 4 - dy, 4)) * 3
+        arriving[slot].wait_recv()
+        onward.append(copy(out_ref.at[pl.ds(theirs, 3)], out_ref.at[pl.ds(theirs, 3)], partner))
+    for c in onward:
+        c.wait_recv()
+    for c in started:
+        c.wait_send()
 
 
 def total_grams(gram):
     def buf(*shape):
         return pltpu.VMEM((*shape, 8, F), jnp.float32)
+
+    def low(n):
+        return pltpu.VMEM((n, 4, F), jnp.float32)
 
     return pl.pallas_call(
         total_body,
@@ -307,10 +331,10 @@
         in_specs=[VM],
         out_specs=(VM, VM),
         scratch_shapes=[
-            buf(96), buf(48), buf(48), buf(3, 12), buf(12), buf(3, 3), buf(8, 3), buf(2), buf(4), buf(4), buf(8),
-            pltpu.SemaphoreType.DMA((35,)), pltpu.SemaphoreType.DMA((35,)),
+            buf(96), buf(48), buf(48), buf(15, 3), buf(8, 3), low(2), low(16), low(8),
+            pltpu.SemaphoreType.DMA((80,)), pltpu.SemaphoreType.DMA((80,)),
         ],
-        compiler_params=pltpu.CompilerParams(collective_id=1, has_side_effects=True, vmem_limit_bytes=16 * 1024 * 1024),
+        compiler_params=pltpu.CompilerParams(collective_id=1, has_side_effects=True, vmem_limit_bytes=12 * 1024 * 1024),
         cost_estimate=pl.CostEstimate(flops=10**6, bytes_accessed=2 * 10**6, transcendentals=0),
         name="total_grams",
     )(gram)
@@ -381,11 +405,11 @@
     own_second = second_hops(1)
     sent = forward(edges)
     chunk(1)
+    chunk(2)
     for c in own_second + far_first:
         c.wait_recv()
     far_second = second_hops(far)
     sent = sent + forward(corners)
-    chunk(2)
     chunk(3)
     for c in [z_near] + far_second + sent:
         c.wait_recv()
@@ -400,7 +424,7 @@
         in_specs=[VM] * 4,
         out_specs=(VM, VM),
         scratch_shapes=[pltpu.VMEM((1024, 256), jnp.float32), pltpu.SemaphoreType.DMA((26,)), pltpu.SemaphoreType.DMA((26,))],
-        compiler_params=pltpu.CompilerParams(collective_id=2, has_side_effects=True, vmem_limit_bytes=BIG),
+        compiler_params=pltpu.CompilerParams(collective_id=2, has_side_effects=True, vmem_limit_bytes=16 * 1024 * 1024),
         cost_estimate=pl.CostEstimate(flops=8 * 10**9, bytes_accessed=3 * 10**6, transcendentals=0),
         name="near_and_counts",
     )(pairs, live, basis, coords)
@@ -412,28 +436,69 @@
 
 NT = ((1,), (1,))
 NN = ((1,), (0,))
+
+
+def cut(x):
+    high = x.astype(jnp.bfloat16)
+    rest = x - high.astype(jnp.float32)
+    mid = rest.astype(jnp.bfloat16)
+    return high, mid, (rest - mid.astype(jnp.float32)).astype(jnp.bfloat16)
+
+
+def outer(p, q):
+    ph, pm, pl_ = cut(p)
+    qh, qm, ql = cut(q)
+    left = jnp.concatenate([ph, ph, pm, ph, pl_, pm], axis=0)
+    right = jnp.concatenate([qh, qm, qh, ql, qh, qm], axis=0)
+    return lax.dot_general(left, right, (((0,), (0,)), ((), ())), preferred_element_type=jnp.float32)
 
 
 def eliminate(mats):
     sub = lax.broadcasted_iota(jnp.int32, (8, F), 0)
     lane = lax.broadcasted_iota(jnp.int32, (8, F), 1)
     tiles = [[m[8 * t : 8 * t + 8, :] for t in range(16)] for m in mats]
-    for j in range(F):
-        t, r = divmod(j, 8)
-        at = lane == j
+
+    def columns(tile, t):
+        return [jnp.broadcast_to(tile[:, 8 * t + k : 8 * t + k + 1], (8, F)) for k in range(8)]
+
+    def spread(tile, r):
+        return jnp.broadcast_to(tile[r : r + 1, :], (8, F))
+
+    for t in range(16):
+        inside = (lane >= 8 * t) & (lane < 8 * t + 8)
         for rows in tiles:
-            pivot = rows[t]
-            inv = 1.0 / jnp.broadcast_to(pivot[r : r + 1, j : j + 1], (8, F))
-            scaled = jnp.where(at, 1.0, jnp.broadcast_to(pivot[r : r + 1, :], (8, F))) * inv
-            for u in range(t, 16):
-                col = jnp.broadcast_to(rows[u][:, j : j + 1], (8, F))
-                if u == t:
-                    if r == 7:
-                        continue
-                    below = sub > r
-                    rows[u] = jnp.where(at & below, 0.0, rows[u]) - jnp.where(below, col, 0.0) * scaled
-                else:
-                    rows[u] = jnp.where(at, 0.0, rows[u]) - col * scaled
+            top = rows[t]
+            c = columns(top, t)
+            lead = t + 1 < 16
+            if lead:
+                after = rows[t + 1]
+                ca = columns(after, t)
+            scaled = []
+            for j in range(8):
+                at = lane == 8 * t + j
+                pivot = [spread(c[k], j) for k in range(j, 8)]
+                inv = 1.0 / pivot[0]
+                row = jnp.where(at, 1.0, spread(top, j))
+                scaled.append(row * inv)
+                if j < 7:
+                    f = jnp.where(sub > j, c[j] * inv, 0.0)
+                    for k in range(j + 1, 8):
+                        c[k] = c[k] - f * pivot[k - j]
+                    top = jnp.where(at & (sub > j), 0.0, top) - f * row
+                if lead:
+                    fa = ca[j] * inv
+                    for k in range(j + 1, 8):
+                        ca[k] = ca[k] - fa * pivot[k - j]
+                    after = jnp.where(at, 0.0, after) - fa * row
+            rows[t] = top
+            if lead:
+                rows[t + 1] = after
+            if t + 2 < 16:
+                packed = jnp.concatenate([s[0:1, :] for s in scaled], axis=0)
+                plain = jnp.where(lane == sub + 8 * t, 1.0, jnp.where(inside & (lane > sub + 8 * t), 0.0, top))
+                taken = outer(packed, plain)
+                for u in range(t + 2, 16):
+                    rows[u] = jnp.where(inside, 0.0, rows[u]) - taken[8 * u : 8 * u + 8, :]
     out = []
     for rows in tiles:
         full = []
@@ -507,7 +572,7 @@
         in_specs=[VM] * 3,
         out_specs=(VM, VM),
         scratch_shapes=[pltpu.VMEM((6, F, F), jnp.float32), pltpu.VMEM((4, F, F), jnp.float32)],
-        compiler_params=pltpu.CompilerParams(vmem_limit_bytes=BIG),
+        compiler_params=pltpu.CompilerParams(vmem_limit_bytes=12 * 1024 * 1024),
         name="solve",
     )(sums, tail, image)
 

time: 133 us -> 93.8 us (0.71)
  Pallas kernels: 130 us -> 89.4 us
    pallas_call x1, Pallas kernels: 40.4 us -> 14.1 us  [solve(): pl.pallas_call(functools.partial(solve_body, total_rows=total_rows), out_...]
    pallas_call x1, Pallas kernels: 30.9 us -> 25.1 us  [near_and_counts(): pl.pallas_call(near_body, out_shape=(jax.ShapeDtypeStruct((4096, F), jnp....]
    pallas_call x1, Pallas kernels: 32.6 us -> 27.8 us  [total_grams(): pl.pallas_call(total_body, out_shape=(jax.ShapeDtypeStruct((96, 8, F), jn...]
    pallas_call x1, Pallas kernels: 25.9 us -> 22.3 us  [apply_pairs(): pl.pallas_call(apply_body, out_shape=(jax.ShapeDtypeStruct((6 * F, K), jn...]
    unnamed x6 -> x12, local copies, waits for them, and re-layouts: 2.47 us -> 3.51 us
where the time goes in v3:
time: 93.8 us; the launch traced here: 93.6 us
  Pallas kernels  89.4 us (95%)
  local copies, waits for them, and re-layouts  3.51 us (4%)
    pallas_call x1, Pallas kernels, total_grams(): pl.pallas_call(total_body, out_shape=(jax.ShapeDtypeStruct((96, 8, F), jn...  27.8 us
    pallas_call x1, Pallas kernels, near_and_counts(): pl.pallas_call(near_body, out_shape=(jax.ShapeDtypeStruct((4096, F), jnp....  25.1 us
    pallas_call x1, Pallas kernels, apply_pairs(): pl.pallas_call(apply_body, out_shape=(jax.ShapeDtypeStruct((6 * F, K), jn...  22.3 us
    pallas_call x1, Pallas kernels, solve(): pl.pallas_call(functools.partial(solve_body, total_rows=total_rows), out_...  14.1 us
    unnamed x12, local copies, waits for them, and re-layouts  3.51 us

profile of v3, /device:TPU:1, one launch (start us, length us, event | category | flops | bytes accessed | tf_op | source)
XLA Modules:
  0.0 93.6 jit_solution(12409934107402404368)
XLA Ops:
  0.6 0.0 copy-start
  0.6 1.0 %copy-done = bf16[1,1,1,128,1536]{4,3,2,1,0:T(8,128)(2,1)S(1)} copy-done((bf16[1,1,1,128,1536]{4,3,2,1,0:T(8,128)(2,1)S(1)}, bf16[1,1,1,128,1536]{4,3,2,1,0:T(8,128)(2,1)}, u32[]{:S(2)}) %copy-start) | copy-done | bytes 393240
  1.6 0.0 copy-start.1
  1.6 0.9 %copy-done.1 = s32[1,1,1,4,15360]{4,3,2,1,0:T(4,128)S(1)} copy-done((s32[1,1,1,4,15360]{4,3,2,1,0:T(4,128)S(1)}, s32[1,1,1,4,15360]{4,3,2,1,0:T(4,128)}, u32[]{:S(2)}) %copy-start.1) | copy-done | bytes 245784
  2.6 0.0 copy-start.2
  2.6 0.8 copy-done.2
  3.4 0.0 copy-start.3
  3.4 0.7 copy-done.3
  4.1 0.0 copy-start.4
  4.1 0.0 copy-start.5
  4.1 25.1 %near_and_counts.1 = (f32[4096,128]{1,0:T(8,128)S(1)}, bf16[992,1792]{1,0:T(8,128)(2,1)S(1)}) custom-call(s32[4,15360]{1,0:T(4,128)S(1)} %bitcast.7, s32[1,15360]{1,0:T(1,128)S(1)} %bitcast.8, bf16[128,1536]{1,0:T(8,128)(2,1)S(1)} %bitcast.6, f32[48,128]{1,0:T(8,128)S(1)} %bitcast.9), custom_call_target="tpu_custom_call" | custom-call | flops 8000000000 | bytes 3000000 | tf_op jit(solution)/shard_map/near_and_counts/pallas_call | solution.py:421
  29.3 0.0 copy-done.4
  29.3 0.0 copy-done.5
  29.3 22.3 %apply_pairs.1 = (f32[768,256]{1,0:T(8,128)S(1)}, f32[768,256]{1,0:T(8,128)S(1)}) custom-call(f32[4096,128]{1,0:T(8,128)S(1)} %get-tuple-element.10.hist_ref, bf16[992,1792]{1,0:T(8,128)(2,1)S(1)} %get-tuple-element.11.table_ref, s32[16,128]{1,0:T(8,128)S(1)} %bitcast.11, f32[48,128]{1,0:T(8,128)S(1)} %bitcast.10), custom_call_target="tpu_custom_call" | custom-call | flops 8000000000 | bytes 8000000 | tf_op jit(solution)/shard_map/apply_pairs/pallas_call | solution.py:190
  51.7 27.8 %total_grams.1 = (f32[96,8,128]{2,1,0:T(8,128)S(1)}, f32[8,128]{1,0:T(8,128)S(1)}) custom-call(f32[768,256]{1,0:T(8,128)S(1)} %get-tuple-element.12.gram_ref), custom_call_target="tpu_custom_call" | custom-call | flops 1000000 | bytes 2000000 | tf_op jit(solution)/shard_map/total_grams/pallas_call | solution.py:328
  79.4 14.1 %solve.1 = (f32[128,1536]{1,0:T(8,128)}, f32[256,256]{1,0:T(8,128)}) custom-call(f32[96,8,128]{2,1,0:T(8,128)S(1)} %get-tuple-element.13.sum_ref, f32[8,128]{1,0:T(8,128)S(1)} %get-tuple-element.14.tail_ref, f32[768,256]{1,0:T(8,128)S(1)} %get-tuple-element.15.image_ref), custom_call_target="tpu_custom_call" | custom-call | tf_op jit(solution)/shard_map/solve/pallas_call | solution.py:569
Async XLA Ops:
  0.6 1.0 %copy-start = (bf16[1,1,1,128,1536]{4,3,2,1,0:T(8,128)(2,1)S(1)}, bf16[1,1,1,128,1536]{4,3,2,1,0:T(8,128)(2,1)}, u32[]{:S(2)}) copy-start(bf16[1,1,1,128,1536]{4,3,2,1,0:T(8,128)(2,1)} %param.9) | copy-start | bytes 1179652
  1.6 0.9 %copy-start.1 = (s32[1,1,1,4,15360]{4,3,2,1,0:T(4,128)S(1)}, s32[1,1,1,4,15360]{4,3,2,1,0:T(4,128)}, u32[]{:S(2)}) copy-start(s32[1,1,1,4,15360]{4,3,2,1,0:T(4,128)} %param.7) | copy-start | bytes 737284
  2.6 0.8 copy-start.2
  3.4 0.7 copy-start.3
  4.1 25.2 %copy-start.4 = (f32[1,1,1,3,16,128]{5,4,3,2,1,0:T(8,128)S(1)}, f32[1,1,1,3,16,128]{5,4,3,2,1,0:T(8,128)}, u32[]{:S(2)}) copy-start(f32[1,1,1,3,16,128]{5,4,3,2,1,0:T(8,128)} %param.5) | copy-start | bytes 73732
  4.1 25.2 %copy-start.5 = (s32[1,1,1,16,128]{4,3,2,1,0:T(8,128)S(1)}, s32[1,1,1,16,128]{4,3,2,1,0:T(8,128)}, u32[]{:S(2)}) copy-start(s32[1,1,1,16,128]{4,3,2,1,0:T(8,128)} %param.6) | copy-start | bytes 24580

commit v4 on v3

--- a/solution.py
+++ b/solution.py
@@ -12,15 +12,14 @@
 NB = 16
 PB = 4096.0
 CHUNK = 3840
-STEP = 768
-
-
-def counter(pairs_ref, live_ref, hist_ref, acc_ref):
-    rows = lax.broadcasted_iota(jnp.int32, (256, STEP), 0)
-    zero = jnp.zeros((256, STEP), jnp.float32)
-
-    def step(at, carry):
-        at = pl.ds(pl.multiple_of(at * STEP, 128), STEP)
+
+
+def counter(pairs_ref, live_ref, hist_ref):
+    rows = lax.broadcasted_iota(jnp.int32, (256, CHUNK), 0)
+    zero = jnp.zeros((256, CHUNK), jnp.float32)
+
+    def chunk(c):
+        at = slice(c * CHUNK, (c + 1) * CHUNK)
         f = pairs_ref[0:1, at]
         s = pairs_ref[1:2, at]
         a = pairs_ref[2:3, at]
@@ -28,23 +27,13 @@
         live = live_ref[0:1, at]
         value = (live * jnp.where(a >= 8, int(PB), 1)).astype(jnp.float32)
         col = ((a >> 2) & 1) * 128 + f
-        right = jnp.where(rows == col, jnp.broadcast_to(value, (256, STEP)), zero).astype(jnp.bfloat16)
+        right = jnp.where(rows == col, jnp.broadcast_to(value, (256, CHUNK)), zero).astype(jnp.bfloat16)
         hot = rows == (b * 16 + s)
         low = a & 3
         for part in range(4):
-            mark = jnp.broadcast_to((low == part).astype(jnp.float32), (256, STEP))
+            mark = jnp.broadcast_to((low == part).astype(jnp.float32), (256, CHUNK))
             left = jnp.where(hot, mark, zero).astype(jnp.bfloat16)
             got = lax.dot_general(left, right, (((1,), (1,)), ((), ())), preferred_element_type=jnp.float32)
-            here = pl.ds(part * 256, 256)
-            acc_ref[here, :] = acc_ref[here, :] + got
-        return carry
-
-    def chunk(c):
-        acc_ref[...] = jnp.zeros_like(acc_ref)
-        steps = CHUNK // STEP
-        lax.fori_loop(c * steps, (c + 1) * steps, step, 0)
-        for part in range(4):
-            got = acc_ref[part * 256 : (part + 1) * 256, :]
             high = jnp.floor(got * (1.0 / PB))
             lower = got - PB * high
             for mid in range(2):
@@ -75,56 +64,66 @@
     return [[six[0], six[1], six[2]], [six[1], six[3], six[4]], [six[2], six[4], six[5]]]
 
 
-def moments(hist_ref, coords_ref, q_ref, blk_ref, rr_ref):
+def moments(hist_ref, coords_ref, q_ref, blk_ref, rr_ref, gather):
     blk_ref[...] = jnp.zeros_like(blk_ref)
     rr_ref[...] = jnp.zeros_like(rr_ref)
     own = [jnp.sum(coords_ref[16 * c : 16 * c + 16, :], axis=0, keepdims=True) * (1.0 / 16.0) for c in range(3)]
+
+    def tile(c, b, half):
+        return q_ref[(c * 16 + b) * 16 + half * 8 : (c * 16 + b) * 16 + half * 8 + 8, :]
+
+    centres = []
     for half in range(2):
-        def tile(c, b):
-            return q_ref[(c * 16 + b) * 16 + half * 8 : (c * 16 + b) * 16 + half * 8 + 8, :]
-
         centre = []
         for c in range(3):
-            total = tile(c, 0)
+            total = tile(c, 0, half)
             for b in range(1, 16):
-                total = total + tile(c, b)
+                total = total + tile(c, b, half)
             centre.append(total * (1.0 / 16.0))
-
-        def atom(a, carry):
-            r = [jnp.broadcast_to(coords_ref[pl.ds(c * 16 + a, 1), :], (8, F)) for c in range(3)]
-            arm = [r[c] - jnp.broadcast_to(own[c], (8, F)) for c in range(3)]
-            m = [None] * 6
-            n = [[None] * 3 for _ in range(3)]
-            for b in range(16):
-                q = [tile(c, b) for c in range(3)]
-                d = [r[c] - q[c] for c in range(3)]
-                count = hist_ref[pl.ds(pl.multiple_of(a * 256 + b * 16 + half * 8, 8), 8), :]
-                w = (0.01 * count) / jnp.maximum(d[0] * d[0] + d[1] * d[1] + d[2] * d[2], 1.0)
-                wd = [w * d[c] for c in range(3)]
-                turn = cross([q[c] - centre[c] for c in range(3)], d)
-                for k, (j, i) in enumerate(SYM):
-                    t = wd[j] * d[i]
-                    m[k] = t if m[k] is None else m[k] + t
-                for j in range(3):
-                    for i in range(3):
-                        t = wd[j] * turn[i]
-                        n[j][i] = t if n[j][i] is None else n[j][i] + t
-            m = symmetric(m)
-            rt = [cross(arm, [m[j][i] for j in range(3)]) for i in range(3)]
-            rn = [cross(arm, [n[j][i] for j in range(3)]) for i in range(3)]
+        centres.append(centre)
+
+    def atom(a, half):
+        centre = centres[half]
+        r = [jnp.broadcast_to(coords_ref[pl.ds(c * 16 + a, 1), :], (8, F)) for c in range(3)]
+        arm = [r[c] - jnp.broadcast_to(own[c], (8, F)) for c in range(3)]
+        m = [None] * 6
+        n = [[None] * 3 for _ in range(3)]
+        for b in range(16):
+            q = [tile(c, b, half) for c in range(3)]
+            d = [r[c] - q[c] for c in range(3)]
+            count = hist_ref[pl.ds(pl.multiple_of(a * 256 + b * 16 + half * 8, 8), 8), :]
+            w = (0.01 * count) / jnp.maximum(d[0] * d[0] + d[1] * d[1] + d[2] * d[2], 1.0)
+            wd = [w * d[c] for c in range(3)]
+            turn = cross([q[c] - centre[c] for c in range(3)], d)
+            for k, (j, i) in enumerate(SYM):
+                t = wd[j] * d[i]
+                m[k] = t if m[k] is None else m[k] + t
             for j in range(3):
                 for i in range(3):
-                    for jj, ii, val in ((j, i, m[j][i]), (j, 3 + i, n[j][i]), (3 + j, i, rt[i][j]), (3 + j, 3 + i, rn[i][j])):
-                        here = pl.ds((jj * 6 + ii) * 16 + half * 8, 8)
-                        blk_ref[here, :] = blk_ref[here, :] - val
-            for j in range(3):
-                rr = cross(arm, [rt[i][j] for i in range(3)])
-                for i in range(3):
-                    here = pl.ds((j * 3 + i) * 8, 8)
-                    rr_ref[here, :] = rr_ref[here, :] + rr[i]
-            return carry
-
-        lax.fori_loop(0, 16, atom, 0)
+                    t = wd[j] * turn[i]
+                    n[j][i] = t if n[j][i] is None else n[j][i] + t
+        m = symmetric(m)
+        rt = [cross(arm, [m[j][i] for j in range(3)]) for i in range(3)]
+        rn = [cross(arm, [n[j][i] for j in range(3)]) for i in range(3)]
+        for j in range(3):
+            for i in range(3):
+                for jj, ii, val in ((j, i, m[j][i]), (j, 3 + i, n[j][i]), (3 + j, i, rt[i][j]), (3 + j, 3 + i, rn[i][j])):
+                    here = pl.ds((jj * 6 + ii) * 16 + half * 8, 8)
+                    blk_ref[here, :] = blk_ref[here, :] - val
+        for j in range(3):
+            rr = cross(arm, [rt[i][j] for i in range(3)])
+            for i in range(3):
+                here = pl.ds((j * 3 + i) * 8, 8)
+                rr_ref[here, :] = rr_ref[here, :] + rr[i]
+
+    def quarter(part, carry):
+        gather(part)
+        for n in range(4):
+            for half in range(2):
+                atom(part * 4 + n, half)
+        return carry
+
+    lax.fori_loop(0, 4, quarter, 0)
     for j in range(3):
         for i in range(3):
             tt = jnp.sum(blk_ref[pl.ds((j * 6 + i) * 16, 16), :], axis=0, keepdims=True)
@@ -141,24 +140,21 @@
 KC = 32
 
 
-def apply_body(hist_ref, table_ref, lists_ref, coords_ref, image_ref, gram_ref, hot_ref, q_ref, g_ref, blk_ref, rr_ref, it_ref, x_ref, y_ref):
-    cols = table_ref.shape[0]
-    for s in range(NB):
-        near = jnp.broadcast_to(lists_ref[s : s + 1, :], (cols, F))
-        hot = lax.broadcasted_iota(jnp.int32, (cols, F), 0) == near
-        hot_ref[:, s * F : (s + 1) * F] = jnp.where(hot, 1.0, 0.0).astype(jnp.bfloat16)
-
-    def gather(lo, hi):
-        return lax.dot_general(table_ref[:, lo:hi], hot_ref[...], (((0,), (0,)), ((), ())), preferred_element_type=jnp.float32)
-
-    got = gather(6 * K, 6 * K + 256)
+def apply_blocks(hist_ref, table_ref, hot_ref, coords_ref, image_ref, q_ref, g_ref, blk_ref, rr_ref, it_ref):
+    def gathered(columns):
+        return lax.dot_general(table_ref[:, columns], hot_ref[...], (((0,), (0,)), ((), ())), preferred_element_type=jnp.float32)
+
+    got = gathered(slice(6 * K, 7 * K))
     pos = got[0:48] + got[48:96] + got[96:144]
     for s in range(NB):
         for t in range(6):
             q_ref[pl.ds(t * 128 + s, 8, stride=16), :] = pos[t * 8 : t * 8 + 8, s * F : (s + 1) * F]
-    moments(hist_ref, coords_ref, q_ref, blk_ref, rr_ref)
-    for i in range(6):
-        g_ref[i * K : (i + 1) * K, :] = gather(i * K, (i + 1) * K)
+
+    def gather(part):
+        at = pl.ds(pl.multiple_of(part * 384, 384), 384)
+        g_ref[at, :] = gathered(at)
+
+    moments(hist_ref, coords_ref, q_ref, blk_ref, rr_ref, gather)
 
     def piece(kc, carry):
         start = pl.multiple_of(kc * KC, KC)
@@ -174,38 +170,8 @@
         return carry
 
     lax.fori_loop(0, K // KC, piece, 0)
-    own = cols - F
     for j in range(6):
-        y = jnp.transpose(it_ref[j * K : (j + 1) * K, :])
-        image_ref[j * F : (j + 1) * F, :] = y
-        y_ref[j * F : (j + 1) * F, :] = y.astype(jnp.bfloat16)
-        x_ref[j * F : (j + 1) * F, :] = table_ref[own:cols, j * K : (j + 1) * K]
-    for n, (p, q) in enumerate(((x_ref, x_ref), (x_ref, y_ref), (y_ref, y_ref))):
-        gram = lax.dot_general(p[...], q[...], (((0,), (0,)), ((), ())), preferred_element_type=jnp.float32)
-        gram_ref[n * K : (n + 1) * K, :] = gram
-
-
-def apply_pairs(hist, table, lists, coords):
-    cols = table.shape[0]
-    return pl.pallas_call(
-        apply_body,
-        out_shape=(jax.ShapeDtypeStruct((6 * F, K), jnp.float32), jax.ShapeDtypeStruct((3 * K, K), jnp.float32)),
-        in_specs=[VM] * 4,
-        out_specs=(VM, VM),
-        scratch_shapes=[
-            pltpu.VMEM((cols, NB * F), jnp.bfloat16),
-            pltpu.VMEM((768, F), jnp.float32),
-            pltpu.VMEM((6 * K, NB * F), jnp.float32),
-            pltpu.VMEM((576, F), jnp.float32),
-            pltpu.VMEM((112, F), jnp.float32),
-            pltpu.VMEM((6 * K, F), jnp.float32),
-            pltpu.VMEM((6 * F, K), jnp.bfloat16),
-            pltpu.VMEM((6 * F, K), jnp.bfloat16),
-        ],
-        compiler_params=pltpu.CompilerParams(vmem_limit_bytes=36 * 1024 * 1024),
-        cost_estimate=pl.CostEstimate(flops=8 * 10**9, bytes_accessed=8 * 10**6, transcendentals=0),
-        name="apply_pairs",
-    )(hist, table, lists, coords)
+        image_ref[j * F : (j + 1) * F, :] = jnp.transpose(it_ref[j * K : (j + 1) * K, :])
 
 
 MESH = pl.DeviceIdType.MESH
@@ -224,7 +190,7 @@
 PLANE = [(dx, dy) for dx in (2, 1, 3, 0) for dy in (2, 1, 3, 0)][:15]
 
 
-def total_body(gram_ref, out_ref, tail_ref, data, half_in, half, plane_in, z_in, t1, t3, t4, send, recv):
+def total_body(image_ref, basis_ref, out_ref, tail_ref, x_ref, y_ref, data, half_in, half, plane_in, z_in, t1, t3, t4, send, recv):
     x, y, z, core = place()
     partner = device(x, y, z, 1 - core)
     plane = [device(lax.rem(x + dx, 4), lax.rem(y + dy, 4), z, core) for dx, dy in PLANE]
@@ -233,16 +199,22 @@
     for peer in [partner] + plane + along_z:
         pl.semaphore_signal(barrier, inc=1, device_id=peer, device_id_type=MESH)
 
+    for j in range(6):
+        x_ref[j * F : (j + 1) * F, :] = basis_ref[:, j * K : (j + 1) * K]
+    y_ref[...] = image_ref[...].astype(jnp.bfloat16)
+
+    def gram(left, right):
+        return lax.dot_general(left[...], right[...], (((0,), (0,)), ((), ())), preferred_element_type=jnp.float32)
+
     lower = lax.broadcasted_iota(jnp.int32, (F, F), 0) >= lax.broadcasted_iota(jnp.int32, (F, F), 1)
     eye = lax.broadcasted_iota(jnp.int32, (F, F), 0) == lax.broadcasted_iota(jnp.int32, (F, F), 1)
     t1[0] = jnp.zeros((4, F), jnp.float32)
     for m in range(3):
-        b11 = gram_ref[m * K : m * K + F, 0:F]
-        b21 = gram_ref[m * K + F : m * K + K, 0:F]
-        b22 = gram_ref[m * K + F : m * K + K, F:K]
+        both = gram(x_ref if m < 2 else y_ref, x_ref if m < 1 else y_ref)
+        b11, b21, b22 = both[:F, :F], both[F:, :F], both[F:, F:]
         if m == 1:
             b11 = b11 + b11.T
-            b21 = b21 + gram_ref[m * K : m * K + F, F:K].T
+            b21 = b21 + both[:F, F:].T
             b22 = b22 + b22.T
         data[m * 32 : m * 32 + 16] = b21.reshape(16, 8, F)
         data[m * 32 + 16 : m * 32 + 32] = jnp.where(lower, b11, b22).reshape(16, 8, F)
@@ -318,7 +290,7 @@
         c.wait_send()
 
 
-def total_grams(gram):
+def total_grams(image, basis):
     def buf(*shape):
         return pltpu.VMEM((*shape, 8, F), jnp.float32)
 
@@ -328,19 +300,39 @@
     return pl.pallas_call(
         total_body,
         out_shape=(jax.ShapeDtypeStruct((96, 8, F), jnp.float32), jax.ShapeDtypeStruct((8, F), jnp.float32)),
-        in_specs=[VM],
+        in_specs=[VM, VM],
         out_specs=(VM, VM),
         scratch_shapes=[
+            pltpu.VMEM((6 * F, K), jnp.bfloat16), pltpu.VMEM((6 * F, K), jnp.bfloat16),
             buf(96), buf(48), buf(48), buf(15, 3), buf(8, 3), low(2), low(16), low(8),
             pltpu.SemaphoreType.DMA((80,)), pltpu.SemaphoreType.DMA((80,)),
         ],
         compiler_params=pltpu.CompilerParams(collective_id=1, has_side_effects=True, vmem_limit_bytes=12 * 1024 * 1024),
         cost_estimate=pl.CostEstimate(flops=10**6, bytes_accessed=2 * 10**6, transcendentals=0),
         name="total_grams",
-    )(gram)
-
-
-def near_body(pairs_ref, live_ref, basis_ref, coords_ref, hist_ref, table_ref, acc_ref, send, recv):
+    )(image, basis)
+
+
+def image_body(
+    pairs_hbm, live_hbm, basis_hbm, coords_hbm, lists_hbm, image_ref,
+    pairs_ref, live_ref, coords_ref, lists_ref, hist_ref, table_ref, hot_ref, q_ref, g_ref, blk_ref, rr_ref, it_ref,
+    loaded, send, recv,
+):
+    own = 27 * 32
+    loads = [
+        pltpu.make_async_copy(src, dst, loaded.at[n])
+        for n, (src, dst) in enumerate(
+            (
+                (coords_hbm, coords_ref),
+                (basis_hbm, table_ref.at[pl.ds(own, F), pl.ds(0, 6 * K)]),
+                (pairs_hbm, pairs_ref),
+                (live_hbm, live_ref),
+                (lists_hbm, lists_ref),
+            )
+        )
+    ]
+    for c in loads:
+        c.start()
     gx, gy, gz = lax.axis_index("gx"), lax.axis_index("gy"), lax.axis_index("gz")
     core = lax.rem(gz, 2)
     far = 2 * core
@@ -352,13 +344,13 @@
     for peer in (partner, beyond, up_x, down_x, up_y, down_y):
         pl.semaphore_signal(barrier, inc=1, device_id=peer, device_id_type=MESH)
 
-    own = 27 * 32
+    loads[0].wait()
     flat = coords_ref[...]
     high = flat.astype(jnp.bfloat16).astype(jnp.float32)
     mid = (flat - high).astype(jnp.bfloat16).astype(jnp.float32)
     parts = jnp.concatenate([high, mid, flat - high - mid, jnp.zeros((112, F), jnp.float32)], axis=0)
-    table_ref[own : own + F, 0 : 6 * K] = basis_ref[...]
     table_ref[own : own + F, 6 * K : 7 * K] = jnp.transpose(parts).astype(jnp.bfloat16)
+    loads[1].wait()
     table_ref[13 * 32 : 14 * 32, :] = table_ref[own : own + 32, :]
     pl.semaphore_wait(barrier, 6)
 
@@ -397,7 +389,9 @@
     z_far = copy(slab(1, 1, 1), slab(1, 1, 2 - far), beyond)
     z_near = copy(slab(1, 1, 1), slab(1, 1, far), partner)
     own_first = first_hops(1)
-    chunk = counter(pairs_ref, live_ref, hist_ref, acc_ref)
+    chunk = counter(pairs_ref, live_ref, hist_ref)
+    loads[2].wait()
+    loads[3].wait()
     chunk(0)
     for c in [z_far] + own_first:
         c.wait_recv()
@@ -405,6 +399,11 @@
     own_second = second_hops(1)
     sent = forward(edges)
     chunk(1)
+    loads[4].wait()
+    for s in range(NB):
+        near = jnp.broadcast_to(lists_ref[s : s + 1, :], (own + F, F))
+        hot = lax.broadcasted_iota(jnp.int32, (own + F, F), 0) == near
+        hot_ref[:, s * F : (s + 1) * F] = jnp.where(hot, 1.0, 0.0).astype(jnp.bfloat16)
     chunk(2)
     for c in own_second + far_first:
         c.wait_recv()
@@ -415,19 +414,37 @@
         c.wait_recv()
     for c in [z_far, z_near] + own_first + far_first + own_second + far_second + sent:
         c.wait_send()
-
-
-def near_and_counts(pairs, live, basis, coords):
+    apply_blocks(hist_ref, table_ref, hot_ref, coords_ref, image_ref, q_ref, g_ref, blk_ref, rr_ref, it_ref)
+
+
+def images(pairs, live, basis, coords, lists):
+    rows = 27 * 32 + F
     return pl.pallas_call(
-        near_body,
-        out_shape=(jax.ShapeDtypeStruct((4096, F), jnp.float32), jax.ShapeDtypeStruct((27 * 32 + F, 7 * K), jnp.bfloat16)),
-        in_specs=[VM] * 4,
-        out_specs=(VM, VM),
-        scratch_shapes=[pltpu.VMEM((1024, 256), jnp.float32), pltpu.SemaphoreType.DMA((26,)), pltpu.SemaphoreType.DMA((26,))],
-        compiler_params=pltpu.CompilerParams(collective_id=2, has_side_effects=True, vmem_limit_bytes=16 * 1024 * 1024),
-        cost_estimate=pl.CostEstimate(flops=8 * 10**9, bytes_accessed=3 * 10**6, transcendentals=0),
-        name="near_and_counts",
-    )(pairs, live, basis, coords)
+        image_body,
+        out_shape=jax.ShapeDtypeStruct((6 * F, K), jnp.float32),
+        in_specs=[pl.BlockSpec(memory_space=pltpu.MemorySpace.HBM)] * 5,
+        out_specs=VM,
+        scratch_shapes=[
+            pltpu.VMEM(pairs.shape, jnp.int32),
+            pltpu.VMEM(live.shape, jnp.int32),
+            pltpu.VMEM((48, F), jnp.float32),
+            pltpu.VMEM((NB, F), jnp.int32),
+            pltpu.VMEM((4096, F), jnp.float32),
+            pltpu.VMEM((rows, 7 * K), jnp.bfloat16),
+            pltpu.VMEM((rows, NB * F), jnp.bfloat16),
+            pltpu.VMEM((768, F), jnp.float32),
+            pltpu.VMEM((6 * K, NB * F), jnp.float32),
+            pltpu.VMEM((576, F), jnp.float32),
+            pltpu.VMEM((112, F), jnp.float32),
+            pltpu.VMEM((6 * K, F), jnp.float32),
+            pltpu.SemaphoreType.DMA((5,)),
+            pltpu.SemaphoreType.DMA((26,)),
+            pltpu.SemaphoreType.DMA((26,)),
+        ],
+        compiler_params=pltpu.CompilerParams(collective_id=2, has_side_effects=True, vmem_limit_bytes=66_000_000),
+        cost_estimate=pl.CostEstimate(flops=16 * 10**9, bytes_accessed=3 * 10**6, transcendentals=0),
+        name="images",
+    )(pairs, live, basis, coords, lists)
 
 
 def dot32(p, q, dims):
@@ -579,9 +596,9 @@
 
 def per_device(coordinates, neighbours, pair_index, pair_live, basis):
     own = coordinates[0, 0, 0].reshape(48, F)
-    hist, table = near_and_counts(pair_index[0, 0, 0], pair_live[0, 0, 0].reshape(1, -1), basis[0, 0, 0], own)
-    image, gram = apply_pairs(hist, table, neighbours[0, 0, 0], own)
-    sums, tail = total_grams(gram)
+    rows = basis[0, 0, 0]
+    image = images(pair_index[0, 0, 0], pair_live[0, 0, 0].reshape(1, -1), rows, own, neighbours[0, 0, 0])
+    sums, tail = total_grams(image, rows)
     next_rows, ritz = solve(sums, tail, image, 6.0 * F * 256)
     return next_rows.reshape(1, 1, 1, F, 6 * K), ritz
 

time: 93.8 us -> 93.4 us (level)
  local copies, waits for them, and re-layouts: 3.51 us -> 1.13 us
  Pallas kernels: 89.4 us -> 91.5 us
    unnamed x12 -> x6, local copies, waits for them, and re-layouts: 3.51 us -> 1.13 us
    pallas_call x2 -> x1, Pallas kernels: 47.5 us -> 49.4 us  [images(): pl.pallas_call(image_body, out_shape=jax.ShapeDtypeStruct((6 * F, K), jnp...]
where the time goes in v4:
time: 93.4 us; the launch traced here: 93.3 us
  Pallas kernels  91.5 us (98%)
  local copies, waits for them, and re-layouts  1.13 us (1%)
    pallas_call x1, Pallas kernels, images(): pl.pallas_call(image_body, out_shape=jax.ShapeDtypeStruct((6 * F, K), jnp...  49.4 us
    pallas_call x1, Pallas kernels, total_grams(): pl.pallas_call(total_body, out_shape=(jax.ShapeDtypeStruct((96, 8, F), jn...  27.9 us
    pallas_call x1, Pallas kernels, solve(): pl.pallas_call(functools.partial(solve_body, total_rows=total_rows), out_...  14.1 us

profile of v4, /device:TPU:1, one launch (start us, length us, event | category | flops | bytes accessed | tf_op | source)
XLA Modules:
  0.0 93.3 jit_solution(5044379528360496010)
XLA Ops:
  0.6 0.0 copy-start.2
  0.6 49.4 %images.1.image_ref = f32[768,256]{1,0:T(8,128)} custom-call(s32[4,15360]{1,0:T(4,128)} %bitcast.9, s32[1,15360]{1,0:T(1,128)} %bitcast.10, bf16[128,1536]{1,0:T(8,128)(2,1)} %bitcast.6, f32[48,128]{1,0:T(8,128)} %bitcast.11, s32[16,128]{1,0:T(8,128)} %bitcast.12), custom_call_target="tpu_custom_call" | custom-call | flops 16000000000 | bytes 3000000 | tf_op jit(solution)/shard_map/images/pallas_call | solution.py:422
  50.1 0.0 copy-done.2
  50.1 0.0 copy-start
  50.1 1.1 %copy-done = f32[768,256]{1,0:T(8,128)S(1)} copy-done((f32[768,256]{1,0:T(8,128)S(1)}, f32[768,256]{1,0:T(8,128)}, u32[]{:S(2)}) %copy-start) | copy-done | bytes 786456
  51.2 0.0 copy-start.1
  51.2 27.9 %total_grams.1 = (f32[96,8,128]{2,1,0:T(8,128)S(1)}, f32[8,128]{1,0:T(8,128)S(1)}) custom-call(f32[768,256]{1,0:T(8,128)S(1)} %copy-done, bf16[128,1536]{1,0:T(8,128)(2,1)S(1)} %bitcast.7), custom_call_target="tpu_custom_call" | custom-call | flops 1000000 | bytes 2000000 | tf_op jit(solution)/shard_map/total_grams/pallas_call | solution.py:300
  79.1 0.0 copy-done.1
  79.2 14.1 %solve.1 = (f32[128,1536]{1,0:T(8,128)}, f32[256,256]{1,0:T(8,128)}) custom-call(f32[96,8,128]{2,1,0:T(8,128)S(1)} %get-tuple-element.6.sum_ref, f32[8,128]{1,0:T(8,128)S(1)} %get-tuple-element.7.tail_ref, f32[768,256]{1,0:T(8,128)S(1)} %copy-done.1), custom_call_target="tpu_custom_call" | custom-call | tf_op jit(solution)/shard_map/solve/pallas_call | solution.py:586
Async XLA Ops:
  0.6 49.4 %copy-start.2 = (bf16[1,1,1,128,1536]{4,3,2,1,0:T(8,128)(2,1)S(1)}, bf16[1,1,1,128,1536]{4,3,2,1,0:T(8,128)(2,1)}, u32[]{:S(2)}) copy-start(bf16[1,1,1,128,1536]{4,3,2,1,0:T(8,128)(2,1)} %param.9) | copy-start | bytes 1179652
  50.1 1.1 %copy-start = (f32[768,256]{1,0:T(8,128)S(1)}, f32[768,256]{1,0:T(8,128)}, u32[]{:S(2)}) copy-start(f32[768,256]{1,0:T(8,128)} %images.1.image_ref) | copy-start | bytes 2359300
  51.2 27.9 %copy-start.1 = (f32[768,256]{1,0:T(8,128)S(1)}, f32[768,256]{1,0:T(8,128)}, u32[]{:S(2)}) copy-start(f32[768,256]{1,0:T(8,128)} %images.1.image_ref) | copy-start | bytes 2359300

commit v5 on v4

--- a/solution.py
+++ b/solution.py
@@ -64,7 +64,7 @@
     return [[six[0], six[1], six[2]], [six[1], six[3], six[4]], [six[2], six[4], six[5]]]
 
 
-def moments(hist_ref, coords_ref, q_ref, blk_ref, rr_ref, gather):
+def moments(hist_ref, coords_ref, q_ref, blk_ref, rr_ref):
     blk_ref[...] = jnp.zeros_like(blk_ref)
     rr_ref[...] = jnp.zeros_like(rr_ref)
     own = [jnp.sum(coords_ref[16 * c : 16 * c + 16, :], axis=0, keepdims=True) * (1.0 / 16.0) for c in range(3)]
@@ -116,14 +116,12 @@
                 here = pl.ds((j * 3 + i) * 8, 8)
                 rr_ref[here, :] = rr_ref[here, :] + rr[i]
 
-    def quarter(part, carry):
-        gather(part)
-        for n in range(4):
-            for half in range(2):
-                atom(part * 4 + n, half)
+    def both(a, carry):
+        for half in range(2):
+            atom(a, half)
         return carry
 
-    lax.fori_loop(0, 4, quarter, 0)
+    lax.fori_loop(0, 16, both, 0)
     for j in range(3):
         for i in range(3):
             tt = jnp.sum(blk_ref[pl.ds((j * 6 + i) * 16, 16), :], axis=0, keepdims=True)
@@ -140,31 +138,37 @@
 KC = 32
 
 
-def apply_blocks(hist_ref, table_ref, hot_ref, coords_ref, image_ref, q_ref, g_ref, blk_ref, rr_ref, it_ref):
-    def gathered(columns):
-        return lax.dot_general(table_ref[:, columns], hot_ref[...], (((0,), (0,)), ((), ())), preferred_element_type=jnp.float32)
-
-    got = gathered(slice(6 * K, 7 * K))
+def chosen(table_ref, columns, hot_ref):
+    return lax.dot_general(table_ref[:, columns], hot_ref[...], (((0,), (0,)), ((), ())), preferred_element_type=jnp.float32)
+
+
+def place_partners(ctab_ref, hot_ref, q_ref):
+    got = chosen(ctab_ref, slice(0, 256), hot_ref)
     pos = got[0:48] + got[48:96] + got[96:144]
     for s in range(NB):
         for t in range(6):
             q_ref[pl.ds(t * 128 + s, 8, stride=16), :] = pos[t * 8 : t * 8 + 8, s * F : (s + 1) * F]
 
-    def gather(part):
-        at = pl.ds(pl.multiple_of(part * 384, 384), 384)
-        g_ref[at, :] = gathered(at)
-
-    moments(hist_ref, coords_ref, q_ref, blk_ref, rr_ref, gather)
+
+def apply_blocks(table_ref, hot_ref, image_ref, g_ref, blk_ref, it_ref):
+    for part in range(6):
+        at = slice(part * K, (part + 1) * K)
+        g_ref[at, :] = chosen(table_ref, at, hot_ref)
 
     def piece(kc, carry):
         start = pl.multiple_of(kc * KC, KC)
-        totals = [jnp.zeros((KC, F), jnp.float32) for _ in range(6)]
-        for s in range(NB):
+
+        def slot(s, totals):
+            totals = list(totals)
+            lanes = pl.ds(pl.multiple_of(s * F, F), F)
             for i in range(6):
-                g = g_ref[pl.ds(i * K + start, KC), s * F : (s + 1) * F]
+                g = g_ref[pl.ds(i * K + start, KC), lanes]
                 for j in range(6):
-                    row = (j * 6 + i) * 16 + s
-                    totals[j] = totals[j] + jnp.broadcast_to(blk_ref[row : row + 1, :], (KC, F)) * g
+                    row = blk_ref[pl.ds((j * 6 + i) * 16 + s, 1), :]
+                    totals[j] = totals[j] + jnp.broadcast_to(row, (KC, F)) * g
+            return tuple(totals)
+
+        totals = lax.fori_loop(0, NB, slot, tuple(jnp.zeros((KC, F), jnp.float32) for _ in range(6)))
         for j in range(6):
             it_ref[pl.ds(j * K + start, KC), :] = totals[j]
         return carry
@@ -190,15 +194,16 @@
 PLANE = [(dx, dy) for dx in (2, 1, 3, 0) for dy in (2, 1, 3, 0)][:15]
 
 
-def total_body(image_ref, basis_ref, out_ref, tail_ref, x_ref, y_ref, data, half_in, half, plane_in, z_in, t1, t3, t4, send, recv):
+def sum_peers():
     x, y, z, core = place()
-    partner = device(x, y, z, 1 - core)
     plane = [device(lax.rem(x + dx, 4), lax.rem(y + dy, 4), z, core) for dx, dy in PLANE]
     along_z = [device(x, y, lax.rem(z + d, 8), core) for d in range(1, 8)]
-    barrier = pltpu.get_barrier_semaphore()
-    for peer in [partner] + plane + along_z:
-        pl.semaphore_signal(barrier, inc=1, device_id=peer, device_id_type=MESH)
-
+    return device(x, y, z, 1 - core), plane, along_z
+
+
+def total_grams(image_ref, basis_ref, out_ref, tail_ref, x_ref, y_ref, data, half_in, half, plane_in, z_in, t1, t3, t4, send, recv):
+    x, y, z, core = place()
+    partner, plane, along_z = sum_peers()
     for j in range(6):
         x_ref[j * F : (j + 1) * F, :] = basis_ref[:, j * K : (j + 1) * K]
     y_ref[...] = image_ref[...].astype(jnp.bfloat16)
@@ -219,8 +224,6 @@
         data[m * 32 : m * 32 + 16] = b21.reshape(16, 8, F)
         data[m * 32 + 16 : m * 32 + 32] = jnp.where(lower, b11, b22).reshape(16, 8, F)
         t1[0, m : m + 1, :] = jnp.sum(jnp.where(eye, b22, 0.0), axis=0, keepdims=True)
-    pl.semaphore_wait(barrier, 23)
-
     count = [0]
     started = []
 
@@ -290,33 +293,10 @@
         c.wait_send()
 
 
-def total_grams(image, basis):
-    def buf(*shape):
-        return pltpu.VMEM((*shape, 8, F), jnp.float32)
-
-    def low(n):
-        return pltpu.VMEM((n, 4, F), jnp.float32)
-
-    return pl.pallas_call(
-        total_body,
-        out_shape=(jax.ShapeDtypeStruct((96, 8, F), jnp.float32), jax.ShapeDtypeStruct((8, F), jnp.float32)),
-        in_specs=[VM, VM],
-        out_specs=(VM, VM),
-        scratch_shapes=[
-            pltpu.VMEM((6 * F, K), jnp.bfloat16), pltpu.VMEM((6 * F, K), jnp.bfloat16),
-            buf(96), buf(48), buf(48), buf(15, 3), buf(8, 3), low(2), low(16), low(8),
-            pltpu.SemaphoreType.DMA((80,)), pltpu.SemaphoreType.DMA((80,)),
-        ],
-        compiler_params=pltpu.CompilerParams(collective_id=1, has_side_effects=True, vmem_limit_bytes=12 * 1024 * 1024),
-        cost_estimate=pl.CostEstimate(flops=10**6, bytes_accessed=2 * 10**6, transcendentals=0),
-        name="total_grams",
-    )(image, basis)
-
-
 def image_body(
-    pairs_hbm, live_hbm, basis_hbm, coords_hbm, lists_hbm, image_ref,
-    pairs_ref, live_ref, coords_ref, lists_ref, hist_ref, table_ref, hot_ref, q_ref, g_ref, blk_ref, rr_ref, it_ref,
-    loaded, send, recv,
+    pairs_hbm, live_hbm, basis_hbm, coords_hbm, lists_hbm, image_ref, sum_ref, tail_ref,
+    pairs_ref, live_ref, coords_ref, lists_ref, hist_ref, table_ref, ctab_ref, hot_ref, q_ref, g_ref, blk_ref, rr_ref, it_ref,
+    x_ref, y_ref, data, half_in, half, plane_in, z_in, t1, t3, t4, loaded, send, recv, sum_send, sum_recv,
 ):
     own = 27 * 32
     loads = [
@@ -324,7 +304,7 @@
         for n, (src, dst) in enumerate(
             (
                 (coords_hbm, coords_ref),
-                (basis_hbm, table_ref.at[pl.ds(own, F), pl.ds(0, 6 * K)]),
+                (basis_hbm, table_ref.at[pl.ds(own, F)]),
                 (pairs_hbm, pairs_ref),
                 (live_hbm, live_ref),
                 (lists_hbm, lists_ref),
@@ -340,8 +320,9 @@
     beyond = {"gz": lax.rem(gz + 7 + 2 * core, 8)}
     up_x, down_x = {"gy": lax.rem(gy + 1, 4)}, {"gy": lax.rem(gy + 3, 4)}
     up_y, down_y = {"gx": lax.rem(gx + 1, 8)}, {"gx": lax.rem(gx + 7, 8)}
+    other, plane, along_z = sum_peers()
     barrier = pltpu.get_barrier_semaphore()
-    for peer in (partner, beyond, up_x, down_x, up_y, down_y):
+    for peer in [partner, beyond, up_x, down_x, up_y, down_y, other] + plane + along_z:
         pl.semaphore_signal(barrier, inc=1, device_id=peer, device_id_type=MESH)
 
     loads[0].wait()
@@ -349,101 +330,150 @@
     high = flat.astype(jnp.bfloat16).astype(jnp.float32)
     mid = (flat - high).astype(jnp.bfloat16).astype(jnp.float32)
     parts = jnp.concatenate([high, mid, flat - high - mid, jnp.zeros((112, F), jnp.float32)], axis=0)
-    table_ref[own : own + F, 6 * K : 7 * K] = jnp.transpose(parts).astype(jnp.bfloat16)
+    ctab_ref[own : own + F, :] = jnp.transpose(parts).astype(jnp.bfloat16)
+    ctab_ref[13 * 32 : 14 * 32, :] = ctab_ref[own : own + 32, :]
     loads[1].wait()
     table_ref[13 * 32 : 14 * 32, :] = table_ref[own : own + 32, :]
-    pl.semaphore_wait(barrier, 6)
+    pl.semaphore_wait(barrier, 29)
 
     count = [0]
-
-    def slab(a, b, e):
-        return table_ref.at[pl.ds(pl.multiple_of((9 * a + 3 * b + e) * 32, 32), 32)]
+    started = []
 
     def copy(src, dst, peer):
         n = count[0]
         count[0] += 1
         c = pltpu.make_async_remote_copy(src_ref=src, dst_ref=dst, send_sem=send.at[n], recv_sem=recv.at[n], device_id=peer, device_id_type=MESH)
         c.start()
+        started.append(c)
         return c
 
-    def first_hops(e):
-        return [
-            copy(slab(1, 1, e), slab(1, 0, e), up_x),
-            copy(slab(1, 1, e), slab(1, 2, e), down_x),
-            copy(slab(1, 1, e), slab(0, 1, e), up_y),
-            copy(slab(1, 1, e), slab(2, 1, e), down_y),
-        ]
-
-    def second_hops(e):
-        return [
-            copy(slab(1, 0, e), slab(0, 0, e), up_y),
-            copy(slab(1, 2, e), slab(2, 2, e), down_y),
-            copy(slab(0, 1, e), slab(0, 2, e), down_x),
-            copy(slab(2, 1, e), slab(2, 0, e), up_x),
-        ]
-
-    def forward(places):
-        return [copy(slab(a, b, 1), slab(a, b, far), partner) for a, b in places]
-
     edges, corners = ((1, 0), (1, 2), (0, 1), (2, 1)), ((0, 0), (2, 2), (0, 2), (2, 0))
-    z_far = copy(slab(1, 1, 1), slab(1, 1, 2 - far), beyond)
-    z_near = copy(slab(1, 1, 1), slab(1, 1, far), partner)
-    own_first = first_hops(1)
+
+    class Ghosts:
+        def __init__(self, ref):
+            self.ref = ref
+
+        def slab(self, a, b, e):
+            return self.ref.at[pl.ds(pl.multiple_of((9 * a + 3 * b + e) * 32, 32), 32)]
+
+        def first_hops(self, e):
+            return [copy(self.slab(1, 1, e), self.slab(a, b, e), peer) for (a, b), peer in zip(edges, (up_x, down_x, up_y, down_y))]
+
+        def second_hops(self, e):
+            return [
+                copy(self.slab(a, b, e), self.slab(c, d, e), peer)
+                for (a, b), (c, d), peer in zip(edges, corners, (up_y, down_y, down_x, up_x))
+            ]
+
+        def forward(self, places):
+            return [copy(self.slab(a, b, 1), self.slab(a, b, far), partner) for a, b in places]
+
+        def one(self):
+            beyond_copy = copy(self.slab(1, 1, 1), self.slab(1, 1, 2 - far), beyond)
+            self.due = [beyond_copy] + self.first_hops(1)
+            self.rest = [copy(self.slab(1, 1, 1), self.slab(1, 1, far), partner)]
+
+        def two(self):
+            for c in self.due:
+                c.wait_recv()
+            self.due = self.first_hops(far) + self.second_hops(1)
+            self.rest = self.rest + self.forward(edges)
+
+        def three(self):
+            for c in self.due:
+                c.wait_recv()
+            self.rest = self.rest + self.second_hops(far) + self.forward(corners)
+
+        def done(self):
+            for c in self.rest:
+                c.wait_recv()
+
+    near, rows = Ghosts(ctab_ref), Ghosts(table_ref)
+    near.one()
+    rows.one()
     chunk = counter(pairs_ref, live_ref, hist_ref)
     loads[2].wait()
     loads[3].wait()
     chunk(0)
-    for c in [z_far] + own_first:
-        c.wait_recv()
-    far_first = first_hops(far)
-    own_second = second_hops(1)
-    sent = forward(edges)
+    near.two()
     chunk(1)
+    near.three()
+    rows.two()
+    chunk(2)
+    chunk(3)
     loads[4].wait()
     for s in range(NB):
-        near = jnp.broadcast_to(lists_ref[s : s + 1, :], (own + F, F))
-        hot = lax.broadcasted_iota(jnp.int32, (own + F, F), 0) == near
+        listed = jnp.broadcast_to(lists_ref[s : s + 1, :], (own + F, F))
+        hot = lax.broadcasted_iota(jnp.int32, (own + F, F), 0) == listed
         hot_ref[:, s * F : (s + 1) * F] = jnp.where(hot, 1.0, 0.0).astype(jnp.bfloat16)
-    chunk(2)
-    for c in own_second + far_first:
-        c.wait_recv()
-    far_second = second_hops(far)
-    sent = sent + forward(corners)
-    chunk(3)
-    for c in [z_near] + far_second + sent:
-        c.wait_recv()
-    for c in [z_far, z_near] + own_first + far_first + own_second + far_second + sent:
+    rows.three()
+    near.done()
+    place_partners(ctab_ref, hot_ref, q_ref)
+    moments(hist_ref, coords_ref, q_ref, blk_ref, rr_ref)
+    rows.done()
+    for c in started:
         c.wait_send()
-    apply_blocks(hist_ref, table_ref, hot_ref, coords_ref, image_ref, q_ref, g_ref, blk_ref, rr_ref, it_ref)
-
-
-def images(pairs, live, basis, coords, lists):
+    apply_blocks(table_ref, hot_ref, image_ref, g_ref, blk_ref, it_ref)
+    total_grams(
+        image_ref, table_ref.at[pl.ds(own, F)], sum_ref, tail_ref, x_ref, y_ref,
+        data, half_in, half, plane_in, z_in, t1, t3, t4, sum_send, sum_recv,
+    )
+
+
+def images_and_sums(pairs, live, basis, coords, lists):
     rows = 27 * 32 + F
+
+    def wide(*shape):
+        return pltpu.VMEM(shape, jnp.float32)
+
+    def half_wide(*shape):
+        return pltpu.VMEM(shape, jnp.bfloat16)
+
+    def semaphores(n):
+        return pltpu.SemaphoreType.DMA((n,))
+
     return pl.pallas_call(
         image_body,
-        out_shape=jax.ShapeDtypeStruct((6 * F, K), jnp.float32),
+        out_shape=(
+            jax.ShapeDtypeStruct((6 * F, K), jnp.float32),
+            jax.ShapeDtypeStruct((96, 8, F), jnp.float32),
+            jax.ShapeDtypeStruct((8, F), jnp.float32),
+        ),
         in_specs=[pl.BlockSpec(memory_space=pltpu.MemorySpace.HBM)] * 5,
-        out_specs=VM,
+        out_specs=(VM, VM, VM),
         scratch_shapes=[
             pltpu.VMEM(pairs.shape, jnp.int32),
             pltpu.VMEM(live.shape, jnp.int32),
-            pltpu.VMEM((48, F), jnp.float32),
+            wide(48, F),
             pltpu.VMEM((NB, F), jnp.int32),
-            pltpu.VMEM((4096, F), jnp.float32),
-            pltpu.VMEM((rows, 7 * K), jnp.bfloat16),
-            pltpu.VMEM((rows, NB * F), jnp.bfloat16),
-            pltpu.VMEM((768, F), jnp.float32),
-            pltpu.VMEM((6 * K, NB * F), jnp.float32),
-            pltpu.VMEM((576, F), jnp.float32),
-            pltpu.VMEM((112, F), jnp.float32),
-            pltpu.VMEM((6 * K, F), jnp.float32),
-            pltpu.SemaphoreType.DMA((5,)),
-            pltpu.SemaphoreType.DMA((26,)),
-            pltpu.SemaphoreType.DMA((26,)),
+            wide(4096, F),
+            half_wide(rows, 6 * K),
+            half_wide(rows, K),
+            half_wide(rows, NB * F),
+            wide(768, F),
+            wide(6 * K, NB * F),
+            wide(576, F),
+            wide(112, F),
+            wide(6 * K, F),
+            half_wide(6 * F, K),
+            half_wide(6 * F, K),
+            wide(96, 8, F),
+            wide(48, 8, F),
+            wide(48, 8, F),
+            wide(15, 3, 8, F),
+            wide(8, 3, 8, F),
+            wide(2, 4, F),
+            wide(16, 4, F),
+            wide(8, 4, F),
+            semaphores(5),
+            semaphores(52),
+            semaphores(52),
+            semaphores(80),
+            semaphores(80),
         ],
         compiler_params=pltpu.CompilerParams(collective_id=2, has_side_effects=True, vmem_limit_bytes=66_000_000),
         cost_estimate=pl.CostEstimate(flops=16 * 10**9, bytes_accessed=3 * 10**6, transcendentals=0),
-        name="images",
+        name="images_and_sums",
     )(pairs, live, basis, coords, lists)
 
 
@@ -528,7 +558,15 @@
     return out
 
 
-def solve_body(sum_ref, tail_ref, image_ref, next_ref, ritz_ref, mat_ref, inv_ref, *, total_rows):
+def solve_body(sum_hbm, tail_hbm, image_hbm, next_ref, ritz_ref, sum_ref, tail_ref, image_ref, mat_ref, inv_ref, loaded, *, total_rows):
+    loads = [
+        pltpu.make_async_copy(src, dst, loaded.at[n])
+        for n, (src, dst) in enumerate(((sum_hbm, sum_ref), (tail_hbm, tail_ref), (image_hbm, image_ref)))
+    ]
+    for c in loads:
+        c.start()
+    loads[0].wait()
+    loads[1].wait()
     scale = 1.0 / total_rows
     sub = lax.broadcasted_iota(jnp.int32, (F, F), 0)
     lane = lax.broadcasted_iota(jnp.int32, (F, F), 1)
@@ -578,6 +616,7 @@
     s_inv = whole(0)
     ritz_ref[...] = dot32(dot32(s_inv, cross_sum, NN), s_inv, NT)
     w_inv = whole(1)
+    loads[2].wait()
     for j in range(6):
         next_ref[:, j * K : (j + 1) * K] = dot32(image_ref[j * F : (j + 1) * F, :], w_inv, NT)
 
@@ -586,19 +625,25 @@
     return pl.pallas_call(
         functools.partial(solve_body, total_rows=total_rows),
         out_shape=(jax.ShapeDtypeStruct((F, 6 * K), jnp.float32), jax.ShapeDtypeStruct((K, K), jnp.float32)),
-        in_specs=[VM] * 3,
+        in_specs=[pl.BlockSpec(memory_space=pltpu.MemorySpace.HBM)] * 3,
         out_specs=(VM, VM),
-        scratch_shapes=[pltpu.VMEM((6, F, F), jnp.float32), pltpu.VMEM((4, F, F), jnp.float32)],
-        compiler_params=pltpu.CompilerParams(vmem_limit_bytes=12 * 1024 * 1024),
+        scratch_shapes=[
+            pltpu.VMEM((96, 8, F), jnp.float32),
+            pltpu.VMEM((8, F), jnp.float32),
+            pltpu.VMEM((6 * F, K), jnp.float32),
+            pltpu.VMEM((6, F, F), jnp.float32),
+            pltpu.VMEM((4, F, F), jnp.float32),
+            pltpu.SemaphoreType.DMA((3,)),
+        ],
+        compiler_params=pltpu.CompilerParams(vmem_limit_bytes=66_000_000),
         name="solve",
     )(sums, tail, image)
 
 
 def per_device(coordinates, neighbours, pair_index, pair_live, basis):
     own = coordinates[0, 0, 0].reshape(48, F)
-    rows = basis[0, 0, 0]
-    image = images(pair_index[0, 0, 0], pair_live[0, 0, 0].reshape(1, -1), rows, own, neighbours[0, 0, 0])
-    sums, tail = total_grams(image, rows)
+    live = pair_live[0, 0, 0].reshape(1, -1)
+    image, sums, tail = images_and_sums(pair_index[0, 0, 0], live, basis[0, 0, 0], own, neighbours[0, 0, 0])
     next_rows, ritz = solve(sums, tail, image, 6.0 * F * 256)
     return next_rows.reshape(1, 1, 1, F, 6 * K), ritz
 

time: 93.4 us -> 83.7 us (0.90)
  Pallas kernels: 91.5 us -> 82.8 us
  local copies, waits for them, and re-layouts: 1.13 us -> 0 us
    pallas_call x2 -> x1, Pallas kernels: 77.3 us -> 67.6 us  [images_and_sums(): pl.pallas_call(image_body, out_shape=(jax.ShapeDtypeStruct((6 * F, K), jn...]
    unnamed x6 -> x0, local copies, waits for them, and re-layouts: 1.13 us -> none
    pallas_call x1, Pallas kernels: 14.1 us -> 15.2 us  [solve(): pl.pallas_call(functools.partial(solve_body, total_rows=total_rows), out_...]
where the time goes in v5:
time: 83.7 us; the launch traced here: 83.6 us
  Pallas kernels  82.8 us (99%)
    pallas_call x1, Pallas kernels, images_and_sums(): pl.pallas_call(image_body, out_shape=(jax.ShapeDtypeStruct((6 * F, K), jn...  67.6 us
    pallas_call x1, Pallas kernels, solve(): pl.pallas_call(functools.partial(solve_body, total_rows=total_rows), out_...  15.2 us

profile of v5, /device:TPU:1, one launch (start us, length us, event | category | flops | bytes accessed | tf_op | source)
XLA Modules:
  0.0 83.6 jit_solution(3974458527503506208)
XLA Ops:
  0.6 67.6 %images_and_sums.1 = (f32[768,256]{1,0:T(8,128)}, f32[96,8,128]{2,1,0:T(8,128)}, f32[8,128]{1,0:T(8,128)}) custom-call(s32[4,15360]{1,0:T(4,128)} %bitcast.8, s32[1,15360]{1,0:T(1,128)} %bitcast.9, bf16[128,1536]{1,0:T(8,128)(2,1)} %bitcast.7, f32[48,128]{1,0:T(8,128)} %bitcast.10, s32[16,128]{1,0:T(8,128)} %bitcast.11), custom_call_target="tpu_custom_call" | custom-call | flops 16000000000 | bytes 3000000 | tf_op jit(solution)/shard_map/images_and_sums/pallas_call | solution.py:435
  68.3 15.2 %solve.1 = (f32[128,1536]{1,0:T(8,128)}, f32[256,256]{1,0:T(8,128)}) custom-call(f32[96,8,128]{2,1,0:T(8,128)} %get-tuple-element.7.sum_hbm, f32[8,128]{1,0:T(8,128)} %get-tuple-element.8.tail_hbm, f32[768,256]{1,0:T(8,128)} %get-tuple-element.9.image_hbm), custom_call_target="tpu_custom_call" | custom-call | tf_op jit(solution)/shard_map/solve/pallas_call | solution.py:625

commit v6 on v5

--- a/solution.py
+++ b/solution.py
@@ -150,11 +150,13 @@
             q_ref[pl.ds(t * 128 + s, 8, stride=16), :] = pos[t * 8 : t * 8 + 8, s * F : (s + 1) * F]
 
 
-def apply_blocks(table_ref, hot_ref, image_ref, g_ref, blk_ref, it_ref):
+def gather_rows(table_ref, hot_ref, g_ref):
     for part in range(6):
         at = slice(part * K, (part + 1) * K)
         g_ref[at, :] = chosen(table_ref, at, hot_ref)
 
+
+def apply_blocks(image_ref, g_ref, blk_ref, it_ref):
     def piece(kc, carry):
         start = pl.multiple_of(kc * KC, KC)
 
@@ -201,29 +203,39 @@
     return device(x, y, z, 1 - core), plane, along_z
 
 
-def total_grams(image_ref, basis_ref, out_ref, tail_ref, x_ref, y_ref, data, half_in, half, plane_in, z_in, t1, t3, t4, send, recv):
-    x, y, z, core = place()
-    partner, plane, along_z = sum_peers()
+def gram(left, right):
+    return lax.dot_general(left[...], right[...], (((0,), (0,)), ((), ())), preferred_element_type=jnp.float32)
+
+
+def basis_gram(basis_ref, x_ref, data):
     for j in range(6):
         x_ref[j * F : (j + 1) * F, :] = basis_ref[:, j * K : (j + 1) * K]
+    both = gram(x_ref, x_ref)
+    for n, block in enumerate((both[F:, :F], both[:F, :F], both[F:, F:], jnp.zeros((F, F), jnp.float32))):
+        data[n * 16 : n * 16 + 16] = block.reshape(16, 8, F)
+
+
+def image_grams(image_ref, x_ref, y_ref, data, tail):
     y_ref[...] = image_ref[...].astype(jnp.bfloat16)
-
-    def gram(left, right):
-        return lax.dot_general(left[...], right[...], (((0,), (0,)), ((), ())), preferred_element_type=jnp.float32)
-
     lower = lax.broadcasted_iota(jnp.int32, (F, F), 0) >= lax.broadcasted_iota(jnp.int32, (F, F), 1)
     eye = lax.broadcasted_iota(jnp.int32, (F, F), 0) == lax.broadcasted_iota(jnp.int32, (F, F), 1)
-    t1[0] = jnp.zeros((4, F), jnp.float32)
-    for m in range(3):
-        both = gram(x_ref if m < 2 else y_ref, x_ref if m < 1 else y_ref)
+    tail[0] = jnp.zeros((4, F), jnp.float32)
+    for m, left in enumerate((x_ref, y_ref)):
+        both = gram(left, y_ref)
         b11, b21, b22 = both[:F, :F], both[F:, :F], both[F:, F:]
-        if m == 1:
+        if m == 0:
             b11 = b11 + b11.T
             b21 = b21 + both[:F, F:].T
             b22 = b22 + b22.T
         data[m * 32 : m * 32 + 16] = b21.reshape(16, 8, F)
         data[m * 32 + 16 : m * 32 + 32] = jnp.where(lower, b11, b22).reshape(16, 8, F)
-        t1[0, m : m + 1, :] = jnp.sum(jnp.where(eye, b22, 0.0), axis=0, keepdims=True)
+        tail[0, m : m + 1, :] = jnp.sum(jnp.where(eye, b22, 0.0), axis=0, keepdims=True)
+
+
+def summing(data, half_in, half, plane_in, z_in, out_ref, send, recv, tails=None):
+    x, y, z, core = place()
+    partner, plane, along_z = sum_peers()
+    here = x * 4 + y
     count = [0]
     started = []
 
@@ -237,56 +249,65 @@
 
     first = []
     for dx in (2, 1, 3, 0):
-        at = lax.rem(x + dx, 4) * 12
-        first.append(copy(data.at[pl.ds((1 - core) * 48 + at, 12)], half_in.at[pl.ds(at, 12)], partner))
-    small = copy(t1.at[0], t1.at[1], partner)
+        at = lax.rem(x + dx, 4) * 8
+        first.append(copy(data.at[pl.ds((1 - core) * 32 + at, 8)], half_in.at[pl.ds(at, 8)], partner))
+    if tails:
+        t1, t3, t4, tail_ref = tails
+        small = copy(t1.at[0], t1.at[1], partner)
+    yield
     arriving = []
     for n, dx in enumerate((2, 1, 3, 0)):
-        at = lax.rem(x + dx, 4) * 12
+        at = lax.rem(x + dx, 4) * 8
         first[n].wait_recv()
-        half[pl.ds(at, 12)] = data[pl.ds(core * 48 + at, 12)] + half_in[pl.ds(at, 12)]
+        half[pl.ds(at, 8)] = data[pl.ds(core * 32 + at, 8)] + half_in[pl.ds(at, 8)]
         for slot, (px, py) in enumerate(PLANE):
             if px == dx:
-                piece = at + lax.rem(y + py, 4) * 3
-                arriving.append(copy(half.at[pl.ds(piece, 3)], plane_in.at[slot], plane[slot]))
-    small.wait_recv()
-    here = x * 4 + y
-    t3[here] = t1[0] + t1[1]
-    tails = [copy(t3.at[here], t3.at[here], plane[slot]) for slot in range(15)]
-    total = half[pl.ds(here * 3, 3)]
+                piece = at + lax.rem(y + py, 4) * 2
+                arriving.append(copy(half.at[pl.ds(piece, 2)], plane_in.at[slot], plane[slot]))
+    if tails:
+        small.wait_recv()
+        t3[here] = t1[0] + t1[1]
+        more = [copy(t3.at[here], t3.at[here], plane[slot]) for slot in range(15)]
+    yield
+    total = half[pl.ds(here * 2, 2)]
     for slot in range(15):
         arriving[slot].wait_recv()
         total = total + plane_in[slot]
     z_in[z] = total
     arriving = [copy(z_in.at[z], z_in.at[z], along_z[d - 1]) for d in range(1, 8)]
-    for c in tails:
-        c.wait_recv()
-    tail = t3[0]
-    for n in range(1, 16):
-        tail = tail + t3[n]
-    t4[z] = tail
-    tails = [copy(t4.at[z], t4.at[z], along_z[d - 1]) for d in range(1, 8)]
+    if tails:
+        for c in more:
+            c.wait_recv()
+        tail = t3[0]
+        for n in range(1, 16):
+            tail = tail + t3[n]
+        t4[z] = tail
+        more = [copy(t4.at[z], t4.at[z], along_z[d - 1]) for d in range(1, 8)]
+    yield
     for c in arriving:
         c.wait_recv()
     total = z_in[0]
     for n in range(1, 8):
         total = total + z_in[n]
-    mine = core * 48 + here * 3
-    out_ref[pl.ds(mine, 3)] = total
-    arriving = [copy(out_ref.at[pl.ds(mine, 3)], out_ref.at[pl.ds(mine, 3)], plane[slot]) for slot in range(15)]
-    onward = [copy(out_ref.at[pl.ds(mine, 3)], out_ref.at[pl.ds(mine, 3)], partner)]
-    for c in tails:
-        c.wait_recv()
-    tail = t4[0]
-    for n in range(1, 8):
-        tail = tail + t4[n]
-    tail_ref[0:4, :] = tail
-    tail_ref[4:8, :] = tail
+    mine = core * 32 + here * 2
+    out_ref[pl.ds(mine, 2)] = total
+    arriving = [copy(out_ref.at[pl.ds(mine, 2)], out_ref.at[pl.ds(mine, 2)], plane[slot]) for slot in range(15)]
+    onward = [copy(out_ref.at[pl.ds(mine, 2)], out_ref.at[pl.ds(mine, 2)], partner)]
+    if tails:
+        for c in more:
+            c.wait_recv()
+        tail = t4[0]
+        for n in range(1, 8):
+            tail = tail + t4[n]
+        tail_ref[0:4, :] = tail
+        tail_ref[4:8, :] = tail
+    yield
     for slot in reversed(range(15)):
         dx, dy = PLANE[slot]
-        theirs = core * 48 + (lax.rem(x + 4 - dx, 4) * 4 + lax.rem(y + 4 - dy, 4)) * 3
+        theirs = core * 32 + (lax.rem(x + 4 - dx, 4) * 4 + lax.rem(y + 4 - dy, 4)) * 2
         arriving[slot].wait_recv()
-        onward.append(copy(out_ref.at[pl.ds(theirs, 3)], out_ref.at[pl.ds(theirs, 3)], partner))
+        onward.append(copy(out_ref.at[pl.ds(theirs, 2)], out_ref.at[pl.ds(theirs, 2)], partner))
+    yield
     for c in onward:
         c.wait_recv()
     for c in started:
@@ -294,9 +315,10 @@
 
 
 def image_body(
-    pairs_hbm, live_hbm, basis_hbm, coords_hbm, lists_hbm, image_ref, sum_ref, tail_ref,
+    pairs_hbm, live_hbm, basis_hbm, coords_hbm, lists_hbm, image_ref, basis_sum_ref, sum_ref, tail_ref,
     pairs_ref, live_ref, coords_ref, lists_ref, hist_ref, table_ref, ctab_ref, hot_ref, q_ref, g_ref, blk_ref, rr_ref, it_ref,
-    x_ref, y_ref, data, half_in, half, plane_in, z_in, t1, t3, t4, loaded, send, recv, sum_send, sum_recv,
+    x_ref, y_ref, basis_data, basis_half_in, basis_half, basis_plane_in, basis_z_in, data, half_in, half, plane_in, z_in, t1, t3, t4,
+    loaded, send, recv, basis_send, basis_recv, sum_send, sum_recv,
 ):
     own = 27 * 32
     loads = [
@@ -334,6 +356,11 @@
     ctab_ref[13 * 32 : 14 * 32, :] = ctab_ref[own : own + 32, :]
     loads[1].wait()
     table_ref[13 * 32 : 14 * 32, :] = table_ref[own : own + 32, :]
+    basis_gram(table_ref.at[pl.ds(own, F)], x_ref, basis_data)
+    chunk = counter(pairs_ref, live_ref, hist_ref)
+    loads[2].wait()
+    loads[3].wait()
+    chunk(0)
     pl.semaphore_wait(barrier, 29)
 
     count = [0]
@@ -391,33 +418,41 @@
     near, rows = Ghosts(ctab_ref), Ghosts(table_ref)
     near.one()
     rows.one()
-    chunk = counter(pairs_ref, live_ref, hist_ref)
-    loads[2].wait()
-    loads[3].wait()
-    chunk(0)
+    basis_sum = summing(
+        basis_data, basis_half_in, basis_half, basis_plane_in, basis_z_in, basis_sum_ref, basis_send, basis_recv
+    )
+    next(basis_sum)
+    chunk(1)
     near.two()
-    chunk(1)
+    chunk(2)
     near.three()
     rows.two()
-    chunk(2)
     chunk(3)
     loads[4].wait()
     for s in range(NB):
         listed = jnp.broadcast_to(lists_ref[s : s + 1, :], (own + F, F))
         hot = lax.broadcasted_iota(jnp.int32, (own + F, F), 0) == listed
         hot_ref[:, s * F : (s + 1) * F] = jnp.where(hot, 1.0, 0.0).astype(jnp.bfloat16)
-    rows.three()
     near.done()
     place_partners(ctab_ref, hot_ref, q_ref)
+    rows.three()
+    next(basis_sum)
     moments(hist_ref, coords_ref, q_ref, blk_ref, rr_ref)
+    next(basis_sum)
     rows.done()
     for c in started:
         c.wait_send()
-    apply_blocks(table_ref, hot_ref, image_ref, g_ref, blk_ref, it_ref)
-    total_grams(
-        image_ref, table_ref.at[pl.ds(own, F)], sum_ref, tail_ref, x_ref, y_ref,
-        data, half_in, half, plane_in, z_in, t1, t3, t4, sum_send, sum_recv,
-    )
+    gather_rows(table_ref, hot_ref, g_ref)
+    next(basis_sum)
+    apply_blocks(image_ref, g_ref, blk_ref, it_ref)
+    image_grams(image_ref, x_ref, y_ref, data, t1)
+    sums = summing(data, half_in, half, plane_in, z_in, sum_ref, sum_send, sum_recv, (t1, t3, t4, tail_ref))
+    next(sums)
+    next(basis_sum)
+    for _ in sums:
+        pass
+    for _ in basis_sum:
+        pass
 
 
 def images_and_sums(pairs, live, basis, coords, lists):
@@ -436,11 +471,12 @@
         image_body,
         out_shape=(
             jax.ShapeDtypeStruct((6 * F, K), jnp.float32),
-            jax.ShapeDtypeStruct((96, 8, F), jnp.float32),
+            jax.ShapeDtypeStruct((64, 8, F), jnp.float32),
+            jax.ShapeDtypeStruct((64, 8, F), jnp.float32),
             jax.ShapeDtypeStruct((8, F), jnp.float32),
         ),
         in_specs=[pl.BlockSpec(memory_space=pltpu.MemorySpace.HBM)] * 5,
-        out_specs=(VM, VM, VM),
+        out_specs=(VM, VM, VM, VM),
         scratch_shapes=[
             pltpu.VMEM(pairs.shape, jnp.int32),
             pltpu.VMEM(live.shape, jnp.int32),
@@ -457,17 +493,15 @@
             wide(6 * K, F),
             half_wide(6 * F, K),
             half_wide(6 * F, K),
-            wide(96, 8, F),
-            wide(48, 8, F),
-            wide(48, 8, F),
-            wide(15, 3, 8, F),
-            wide(8, 3, 8, F),
+            *([wide(64, 8, F), wide(32, 8, F), wide(32, 8, F), wide(15, 2, 8, F), wide(8, 2, 8, F)] * 2),
             wide(2, 4, F),
             wide(16, 4, F),
             wide(8, 4, F),
             semaphores(5),
             semaphores(52),
             semaphores(52),
+            semaphores(57),
+            semaphores(57),
             semaphores(80),
             semaphores(80),
         ],
@@ -558,15 +592,17 @@
     return out
 
 
-def solve_body(sum_hbm, tail_hbm, image_hbm, next_ref, ritz_ref, sum_ref, tail_ref, image_ref, mat_ref, inv_ref, loaded, *, total_rows):
+def solve_body(basis_hbm, sum_hbm, tail_hbm, image_hbm, next_ref, ritz_ref, basis_ref, sum_ref, tail_ref, image_ref, mat_ref, inv_ref, loaded, *, total_rows):
     loads = [
         pltpu.make_async_copy(src, dst, loaded.at[n])
-        for n, (src, dst) in enumerate(((sum_hbm, sum_ref), (tail_hbm, tail_ref), (image_hbm, image_ref)))
+        for n, (src, dst) in enumerate(
+            ((basis_hbm, basis_ref), (sum_hbm, sum_ref), (tail_hbm, tail_ref), (image_hbm, image_ref))
+        )
     ]
     for c in loads:
         c.start()
-    loads[0].wait()
-    loads[1].wait()
+    for c in loads[:3]:
+        c.wait()
     scale = 1.0 / total_rows
     sub = lax.broadcasted_iota(jnp.int32, (F, F), 0)
     lane = lax.broadcasted_iota(jnp.int32, (F, F), 1)
@@ -580,8 +616,8 @@
         b22 = jnp.where(sub < lane, both, jnp.where(sub == lane, diag, flip))
         return b11, b21, b22
 
-    s11, s21, s22 = unpack(0, scale)
-    w11, w21, w22 = unpack(2, scale)
+    s21, s11, s22 = [basis_ref[n * 16 : n * 16 + 16].reshape(F, F) * scale for n in range(3)]
+    w11, w21, w22 = unpack(1, scale)
     mat_ref[0] = s11
     mat_ref[1] = w11
     for n, (b21, b22) in enumerate(((s21, s22), (w21, w22))):
@@ -611,40 +647,41 @@
             [jnp.concatenate([top, jnp.zeros((F, F), jnp.float32)], axis=1), jnp.concatenate([corner, low], axis=1)], axis=0
         )
 
-    q11, q21, q22 = unpack(1, 0.5 * scale)
+    q11, q21, q22 = unpack(0, 0.5 * scale)
     cross_sum = jnp.concatenate([jnp.concatenate([q11, q21.T], axis=1), jnp.concatenate([q21, q22], axis=1)], axis=0)
     s_inv = whole(0)
     ritz_ref[...] = dot32(dot32(s_inv, cross_sum, NN), s_inv, NT)
     w_inv = whole(1)
-    loads[2].wait()
+    loads[3].wait()
     for j in range(6):
         next_ref[:, j * K : (j + 1) * K] = dot32(image_ref[j * F : (j + 1) * F, :], w_inv, NT)
 
 
-def solve(sums, tail, image, total_rows):
+def solve(basis_sum, sums, tail, image, total_rows):
     return pl.pallas_call(
         functools.partial(solve_body, total_rows=total_rows),
         out_shape=(jax.ShapeDtypeStruct((F, 6 * K), jnp.float32), jax.ShapeDtypeStruct((K, K), jnp.float32)),
-        in_specs=[pl.BlockSpec(memory_space=pltpu.MemorySpace.HBM)] * 3,
+        in_specs=[pl.BlockSpec(memory_space=pltpu.MemorySpace.HBM)] * 4,
         out_specs=(VM, VM),
         scratch_shapes=[
-            pltpu.VMEM((96, 8, F), jnp.float32),
+            pltpu.VMEM((64, 8, F), jnp.float32),
+            pltpu.VMEM((64, 8, F), jnp.float32),
             pltpu.VMEM((8, F), jnp.float32),
             pltpu.VMEM((6 * F, K), jnp.float32),
             pltpu.VMEM((6, F, F), jnp.float32),
             pltpu.VMEM((4, F, F), jnp.float32),
-            pltpu.SemaphoreType.DMA((3,)),
+            pltpu.SemaphoreType.DMA((4,)),
         ],
         compiler_params=pltpu.CompilerParams(vmem_limit_bytes=66_000_000),
         name="solve",
-    )(sums, tail, image)
+    )(basis_sum, sums, tail, image)
 
 
 def per_device(coordinates, neighbours, pair_index, pair_live, basis):
     own = coordinates[0, 0, 0].reshape(48, F)
     live = pair_live[0, 0, 0].reshape(1, -1)
-    image, sums, tail = images_and_sums(pair_index[0, 0, 0], live, basis[0, 0, 0], own, neighbours[0, 0, 0])
-    next_rows, ritz = solve(sums, tail, image, 6.0 * F * 256)
+    image, basis_sum, sums, tail = images_and_sums(pair_index[0, 0, 0], live, basis[0, 0, 0], own, neighbours[0, 0, 0])
+    next_rows, ritz = solve(basis_sum, sums, tail, image, 6.0 * F * 256)
     return next_rows.reshape(1, 1, 1, F, 6 * K), ritz
 
 

time: 83.7 us -> 85.3 us (1.019)
  Pallas kernels: 82.8 us -> 84.4 us
    pallas_call x1, Pallas kernels: 67.6 us -> 69.1 us  [images_and_sums(): pl.pallas_call(image_body, out_shape=(jax.ShapeDtypeStruct((6 * F, K), jn...]
where the time goes in v6:
time: 85.3 us; the launch traced here: 85.2 us
  Pallas kernels  84.4 us (99%)
    pallas_call x1, Pallas kernels, images_and_sums(): pl.pallas_call(image_body, out_shape=(jax.ShapeDtypeStruct((6 * F, K), jn...  69.1 us
    pallas_call x1, Pallas kernels, solve(): pl.pallas_call(functools.partial(solve_body, total_rows=total_rows), out_...  15.2 us

profile of v6, /device:TPU:1, one launch (start us, length us, event | category | flops | bytes accessed | tf_op | source)
XLA Modules:
  0.0 85.2 jit_solution(15181872824316357061)
XLA Ops:
  0.6 69.1 %images_and_sums.1 = (f32[768,256]{1,0:T(8,128)}, f32[64,8,128]{2,1,0:T(8,128)}, f32[64,8,128]{2,1,0:T(8,128)}, f32[8,128]{1,0:T(8,128)}) custom-call(s32[4,15360]{1,0:T(4,128)} %bitcast.8, s32[1,15360]{1,0:T(1,128)} %bitcast.9, bf16[128,1536]{1,0:T(8,128)(2,1)} %bitcast.7, f32[48,128]{1,0:T(8,128)} %bitcast.10, s32[16,128]{1,0:T(8,128)} %bitcast.11), custom_call_target="tpu_custom_call" | custom-call | flops 16000000000 | bytes 3000000 | tf_op jit(solution)/shard_map/images_and_sums/pallas_call | solution.py:470
  69.7 15.2 %solve.1 = (f32[128,1536]{1,0:T(8,128)}, f32[256,256]{1,0:T(8,128)}) custom-call(f32[64,8,128]{2,1,0:T(8,128)} %get-tuple-element.8.basis_hbm, f32[64,8,128]{2,1,0:T(8,128)} %get-tuple-element.9.sum_hbm, f32[8,128]{1,0:T(8,128)} %get-tuple-element.10.tail_hbm, f32[768,256]{1,0:T(8,128)} %get-tuple-element.11.image_hbm), custom_call_target="tpu_custom_call" | custom-call | tf_op jit(solution)/shard_map/solve/pallas_call | solution.py:661

commit v7 on v5

--- a/solution.py
+++ b/solution.py
@@ -168,7 +168,7 @@
                     totals[j] = totals[j] + jnp.broadcast_to(row, (KC, F)) * g
             return tuple(totals)
 
-        totals = lax.fori_loop(0, NB, slot, tuple(jnp.zeros((KC, F), jnp.float32) for _ in range(6)))
+        totals = lax.fori_loop(0, NB, slot, tuple(jnp.zeros((KC, F), jnp.float32) for _ in range(6)), unroll=2)
         for j in range(6):
             it_ref[pl.ds(j * K + start, KC), :] = totals[j]
         return carry

time: 83.7 us -> 83.1 us (level)
  no operation moved by 1% of the time
where the time goes in v7:
time: 83.1 us; the launch traced here: 83 us
  Pallas kernels  82.2 us (99%)
    pallas_call x1, Pallas kernels, images_and_sums(): pl.pallas_call(image_body, out_shape=(jax.ShapeDtypeStruct((6 * F, K), jn...  67 us
    pallas_call x1, Pallas kernels, solve(): pl.pallas_call(functools.partial(solve_body, total_rows=total_rows), out_...  15.2 us

profile of v7, /device:TPU:1, one launch (start us, length us, event | category | flops | bytes accessed | tf_op | source)
XLA Modules:
  0.0 83.0 jit_solution(11068505891013613848)
XLA Ops:
  0.6 67.0 %images_and_sums.1 = (f32[768,256]{1,0:T(8,128)}, f32[96,8,128]{2,1,0:T(8,128)}, f32[8,128]{1,0:T(8,128)}) custom-call(s32[4,15360]{1,0:T(4,128)} %bitcast.8, s32[1,15360]{1,0:T(1,128)} %bitcast.9, bf16[128,1536]{1,0:T(8,128)(2,1)} %bitcast.7, f32[48,128]{1,0:T(8,128)} %bitcast.10, s32[16,128]{1,0:T(8,128)} %bitcast.11), custom_call_target="tpu_custom_call" | custom-call | flops 16000000000 | bytes 3000000 | tf_op jit(solution)/shard_map/images_and_sums/pallas_call | solution.py:435
  67.7 15.2 %solve.1 = (f32[128,1536]{1,0:T(8,128)}, f32[256,256]{1,0:T(8,128)}) custom-call(f32[96,8,128]{2,1,0:T(8,128)} %get-tuple-element.7.sum_hbm, f32[8,128]{1,0:T(8,128)} %get-tuple-element.8.tail_hbm, f32[768,256]{1,0:T(8,128)} %get-tuple-element.9.image_hbm), custom_call_target="tpu_custom_call" | custom-call | tf_op jit(solution)/shard_map/solve/pallas_call | solution.py:625
